TPU v7x, 128 devices: a whole 4x4x4 slice. The times are simulated.
128 devices in a mesh: req: 16 (over y, x_hi, core), tp: 8 (over x_lo, z).
Axes of the slice: x: 4 (x_hi: 2, x_lo: 2; x = x_hi * 2 + x_lo), y: 4, z: 4, core: 2. Of those that a mesh axis runs over, the one named last changes fastest.
Arguments:
- hidden_in: bfloat16 [16384, 7168], P(('req', 'tp')), may hold values from -6 to 6
- ln_gain: float32 [7168], replicated, may hold values from 0.1 to 1.9
- ln_bias: float32 [7168], replicated, may hold values from -3 to 3
- w_query: bfloat16 [7168, 4096], P(None, 'tp'), may hold values from -0.0625 to 0.0625
- w_key: bfloat16 [7168, 4096], P(None, 'tp'), may hold values from -0.0625 to 0.0625
- w_value: bfloat16 [7168, 4096], P(None, 'tp'), may hold values from -0.0625 to 0.0625
- qkv_bias: float32 [3, 4096], P(None, 'tp'), may hold values from -34 to 34
- segment_ids: int32 [16384], P('req'), may hold values from -1 to 19, as said below
- page_table: int32 [1024], P('req'), may hold values from 0 to 1023, as said below
Outputs:
- context: bfloat16 [16384, 4096], P('req', 'tp')
- kv_cache: bfloat16 [2, 32, 1024, 16, 128], P(None, 'tp', 'req')
Inputs may be any that keep to these rules, and one draw needn't show every extreme that they name: `segment_ids`: within each block of 1024 positions, live positions come first and padding (-1) fills the tail; ids count the block's requests from 0 upward, each request contiguous and starting at a multiple of 32 positions within its block. In every draw one block holds a single request of exactly 1024 positions; every other request has at most 256 positions. `page_table`: every slot is named once. Of the 64 pages of one block of 1024 positions, exactly 4 name slots s with s // 64 equal to each given value.
All inputs are finite; a program needn't handle non-finite values.
Results may differ from a plain program's by a relative error of at most 0.012.
The roundings to bfloat16 on the way count: a program that leaves them out, or rounds other values in their place, can miss the bound.
Values may be sent and summed in bfloat16 or wider, within the bound.
A program may use at most 128 MiB of HBM per device.

v0:
```python
import functools

import jax
import jax.numpy as jnp
from jax import lax
from jax.experimental import pallas as pl
from jax.sharding import PartitionSpec as P

HEAD_DIM = 128
SPLIT = 6656
Q_BLOCK = 256


def layer_norm(rows, gain, shift):
    values = rows.astype(jnp.float32)
    center = values - jnp.mean(values, axis=1, keepdims=True)
    spread = jnp.mean(center * center, axis=1, keepdims=True)
    return (center * lax.rsqrt(spread + 1e-05) * gain + shift).astype(jnp.bfloat16)


def attention_kernel(q_ref, k_ref, v_ref, lo_ref, hi_ref, o_ref, *, block):
    qb = pl.program_id(0)
    for b in range(k_ref.shape[0] // block):

        @pl.when(qb == b)
        def _():
            n = (b + 1) * block
            col = lax.broadcasted_iota(jnp.int32, (block, n), 1)
            lo = lo_ref[...]
            hi = hi_ref[...]
            visible = (col >= lo) & (col <= hi)
            live = hi >= 0
            for h in range(q_ref.shape[1] // HEAD_DIM):
                cols = slice(h * HEAD_DIM, (h + 1) * HEAD_DIM)
                scores = lax.dot_general(
                    q_ref[:, cols],
                    k_ref[0:n, cols],
                    (((1,), (1,)), ((), ())),
                    preferred_element_type=jnp.float32,
                )
                scores = jnp.where(visible, scores, -1e30)
                top = jnp.max(scores, axis=1, keepdims=True)
                weights = jnp.exp(scores - top)
                total = jnp.maximum(jnp.sum(weights, axis=1, keepdims=True), 1.0)
                scale = jnp.where(live, 1.0 / total, 0.0)
                probs = (weights * scale).astype(jnp.bfloat16)
                o_ref[:, cols] = jnp.dot(
                    probs, v_ref[0:n, cols], preferred_element_type=jnp.float32
                ).astype(o_ref.dtype)


def attend(query, keys, values, segments):
    positions, width = query.shape
    block = Q_BLOCK
    position = jnp.arange(positions, dtype=jnp.int32)
    first = jnp.concatenate([jnp.ones((1,), bool), segments[1:] != segments[:-1]])
    lo = lax.cummax(jnp.where(first, position, 0), axis=0)
    hi = jnp.where(segments >= 0, position, -1)
    kernel = functools.partial(attention_kernel, block=block)
    return pl.pallas_call(
        kernel,
        grid=(positions // block,),
        in_specs=[
            pl.BlockSpec((block, width), lambda i: (i, 0)),
            pl.BlockSpec((positions, width), lambda i: (0, 0)),
            pl.BlockSpec((positions, width), lambda i: (0, 0)),
            pl.BlockSpec((block, 1), lambda i: (i, 0)),
            pl.BlockSpec((block, 1), lambda i: (i, 0)),
        ],
        out_specs=pl.BlockSpec((block, width), lambda i: (i, 0)),
        out_shape=jax.ShapeDtypeStruct((positions, width), query.dtype),
    )(query, keys, values, lo.reshape(positions, 1), hi.reshape(positions, 1))


def send_pages(keys, values, page_table):
    pages = page_table.shape[0]
    positions, width = keys.shape
    page_rows = positions // pages
    heads = width // HEAD_DIM
    stacked = (
        jnp.stack([keys, values], axis=0)
        .reshape(2, pages, page_rows, heads, HEAD_DIM)
        .transpose(1, 0, 2, 3, 4)
    )
    target = page_table // pages
    local_slot = page_table % pages
    order = jnp.argsort(target, stable=True)
    slots = lax.all_to_all(local_slot[order], "req", split_axis=0, concat_axis=0, tiled=True)
    inverse = jnp.argsort(slots)
    moved = lax.all_to_all(stacked[order], "req", split_axis=0, concat_axis=0, tiled=True)
    return moved[inverse].transpose(1, 3, 0, 2, 4)


def project_chunks(normed_local, w_query, w_key, w_value, qkv_bias, live, bounds):
    sums = [None, None, None]
    for lo, hi in zip(bounds[:-1], bounds[1:]):
        part = lax.all_gather(normed_local[:, lo:hi], "tp", axis=0, tiled=True)
        for i, w in enumerate((w_value, w_key, w_query)):
            term = jnp.dot(part, w[lo:hi], preferred_element_type=jnp.float32)
            sums[2 - i] = term if sums[2 - i] is None else sums[2 - i] + term
        if hi < bounds[-1]:
            sums = list(lax.optimization_barrier(tuple(sums)))
    query = (sums[0] + qkv_bias[0]) * HEAD_DIM ** (-0.5)
    keys = jnp.where(live[:, None], sums[1] + qkv_bias[1], 0.0)
    values = jnp.where(live[:, None], sums[2] + qkv_bias[2], 0.0)
    return (query.astype(jnp.bfloat16), keys.astype(jnp.bfloat16), values.astype(jnp.bfloat16))


def on_device(
    hidden_in, ln_gain, ln_bias, w_query, w_key, w_value, qkv_bias, segment_ids, page_table
):
    bounds = (0, SPLIT, hidden_in.shape[1])
    query, keys, values = project_chunks(
        layer_norm(hidden_in, ln_gain, ln_bias),
        w_query,
        w_key,
        w_value,
        qkv_bias,
        segment_ids >= 0,
        bounds,
    )
    context = attend(query, keys, values, segment_ids)
    kv_cache = send_pages(keys, values, page_table)
    return (context, kv_cache)


def solution(mesh):
    return jax.shard_map(
        on_device,
        mesh=mesh,
        in_specs=(
            P(("req", "tp"), None),
            P(),
            P(),
            P(None, "tp"),
            P(None, "tp"),
            P(None, "tp"),
            P(None, "tp"),
            P("req"),
            P("req"),
        ),
        out_specs=(P("req", "tp"), P(None, "tp", "req", None, None)),
        check_vma=False,
    )
```

profile of v0, /device:TPU:1, one launch (start us, length us, event | category | flops | bytes accessed | tf_op | source)
XLA Modules:
  0.0 256.1 jit_solution(14491265842913429438)
XLA Ops:
  7.2 1.9 convert_reduce_fusion
  10.7 1.2 copy-done.1
  11.9 1.3 slice.67
  13.3 2.0 sort.34
  16.8 8.4 %all-to-all-start.1 = ((s32[16,4,1]{1,2,0:T(1,128)}), s32[16,4,1]{1,2,0:T(1,128)S(1)}, u32[]{:S(2)}, u32[]{:S(2)}) async-start(s32[16,4,1]{1,2,0:T(1,128)} %bitcast.7), calls=%async_computation.1 | async-start | bytes 16384 | tf_op jit(solution)/shard_map/all_to_all | solution.py:88
  25.2 1.6 slice.68
  26.9 130.8 %all-gather.3.cloned.1.call-done = bf16[1024,6656]{1,0:T(8,128)(2,1)} async-done(((bf16[128,6656]{1,0:T(8,128)(2,1)}), bf16[1024,6656]{1,0:T(8,128)(2,1)}) %all-gather.3.cloned.1.call-update) | async-done | bytes 13631504 | tf_op jit(solution)/shard_map/all_gather | solution.py:97
  157.8 12.7 %fusion = f32[1024,512]{1,0:T(8,128)S(1)} fusion(bf16[1024,6656]{1,0:T(8,128)(2,1)} %all-gather.3.cloned.1.call-done, bf16[7168,512]{1,0:T(8,128)(2,1)} %param.14), kind=kOutput, calls=%fused_computation.3 | convolution fusion | flops 6979321856 | bytes 22544384 | tf_op jit(solution)/shard_map/dot_general | solution.py:99
  170.5 10.5 %fusion.2 = f32[1024,512]{1,0:T(8,128)} fusion(bf16[1024,6656]{1,0:T(8,128)(2,1)S(1)} %copy-done.9, bf16[7168,512]{1,0:T(8,128)(2,1)} %param.13), kind=kOutput, calls=%fused_computation.5 | convolution fusion | flops 6979321856 | bytes 22544384 | tf_op jit(solution)/shard_map/dot_general | solution.py:99
  181.0 8.5 %fusion.4 = f32[1024,512]{1,0:T(8,128)} fusion(bf16[1024,6656]{1,0:T(8,128)(2,1)S(1)} %copy-done.9, bf16[7168,512]{1,0:T(8,128)(2,1)S(1)} %bitcast.27), kind=kOutput, calls=%fused_computation.7 | convolution fusion | flops 6979321856 | bytes 22544384 | tf_op jit(solution)/shard_map/dot_general | solution.py:99
  189.5 3.1 %all-gather.5.cloned.1.call-done = bf16[1024,512]{1,0:T(8,128)(2,1)} async-done(((bf16[128,512]{1,0:T(8,128)(2,1)}), bf16[1024,512]{1,0:T(8,128)(2,1)}) %all-gather.5.cloned.1.call-update) | async-done | bytes 1048592 | tf_op jit(solution)/shard_map/all_gather | solution.py:97
  192.6 2.1 select_convert_fusion.v_ref
  195.0 1.2 copy.22
  197.3 1.7 select_convert_fusion.1.k_ref
  200.9 2.2 gather_fusion
  203.1 12.4 %all-to-all-start = ((bf16[64,2,16,4,128]{4,2,3,1,0:T(8,128)(2,1)}), bf16[64,2,16,4,128]{4,2,3,1,0:T(8,128)(2,1)S(1)}, u32[]{:S(2)}, u32[]{:S(2)}) async-start(bf16[64,2,16,4,128]{4,2,3,1,0:T(8,128)(2,1)} %gather_fusion), calls=%async_computation | async-start | bytes 4194304 | tf_op jit(solution)/shard_map/all_to_all | solution.py:90
  216.2 1.0 copy.19.lo_ref
  217.3 1.0 copy.20.hi_ref
  219.6 2.0 sort.35
  221.6 3.5 %multiply_convert_fusion.q_ref = bf16[1024,512]{1,0:T(8,128)(2,1)} fusion(f32[1024,512]{1,0:T(8,128)} %fusion.4, bf16[1024,512]{1,0:T(8,128)(2,1)S(1)} %copy-done.11, f32[512]{0:T(512)S(1)} %bitcast.23, bf16[7168,512]{1,0:T(8,128)(2,1)} %param.12), kind=kOutput, calls=%fused_computation.20 | convolution fusion | flops 538968064 | bytes 4720640 | tf_op jit(solution)/shard_map/dot_general | solution.py:99
  225.1 12.3 %shard_map.104 = bf16[1024,512]{1,0:T(8,128)(2,1)} custom-call(bf16[1024,512]{1,0:T(8,128)(2,1)} %multiply_convert_fusion.q_ref, bf16[1024,512]{1,0:T(8,128)(2,1)} %copy-done.3, bf16[1024,512]{1,0:T(8,128)(2,1)} %copy-done.2, s32[1024,1]{1,0:T(8,128)} %copy.19.lo_ref, s32[1024,1]{1,0:T(8,128)} %copy.20.hi_ref), custom_call_target="tpu_custom_call" | custom-call | tf_op jit(solution)/shard_map/pallas_call | solution.py:60
  237.4 6.4 %all-to-all-done = bf16[64,2,16,4,128]{4,2,3,1,0:T(8,128)(2,1)S(1)} async-done(((bf16[64,2,16,4,128]{4,2,3,1,0:T(8,128)(2,1)}), bf16[64,2,16,4,128]{4,2,3,1,0:T(8,128)(2,1)S(1)}, u32[]{:S(2)}, u32[]{:S(2)}) %all-to-all-start) | async-done | bytes 2097184 | tf_op jit(solution)/shard_map/all_to_all | solution.py:90
  243.8 2.2 gather_fusion.2
  246.0 3.3 %copy.24 = bf16[2,4,64,16,128]{4,3,2,1,0:T(8,128)(2,1)} copy(bf16[2,4,64,16,128]{4,3,1,0,2:T(8,128)(2,1)} %bitcast.20) | data formatting | bytes 4194304
  (66 shorter events, 8.3 us)
Async XLA Ops:
  7.2 2.1 copy-start
  7.2 2.7 %copy-start.7 = (f32[7168]{0:T(1024)S(1)}, f32[7168]{0:T(1024)}, u32[]{:S(2)}) copy-start(f32[7168]{0:T(1024)} %param.10) | copy-start | bytes 86020
  7.2 2.7 %copy-start.6 = (f32[7168]{0:T(1024)S(1)}, f32[7168]{0:T(1024)}, u32[]{:S(2)}) copy-start(f32[7168]{0:T(1024)} %param.11) | copy-start | bytes 86020
  7.2 150.6 %all-gather.3.cloned.1.call-start = ((), (), s32[]{:S(2)}) async-start(), calls=%async_computation.2 | async-start | bytes 15335424 | tf_op jit(solution)/shard_map/all_gather | solution.py:97
  10.7 1.2 copy-start.1
  11.9 1.3 copy-start.12
  13.2 13.7 %copy-start.8 = (f32[3,512]{1,0:T(4,128)S(1)}, f32[3,512]{1,0:T(4,128)}, u32[]{:S(2)}) copy-start(f32[3,512]{1,0:T(4,128)} %param.15) | copy-start | bytes 18436
  13.2 13.7 %copy-start.5 = (s32[1024]{0:T(1024)S(1)}, s32[1024]{0:T(1024)}, u32[]{:S(2)}) copy-start(s32[1024]{0:T(1024)} %param.16) | copy-start | bytes 12292
  16.8 186.3 %all-to-all-start.1 = ((s32[16,4,1]{1,2,0:T(1,128)}), s32[16,4,1]{1,2,0:T(1,128)S(1)}, u32[]{:S(2)}, u32[]{:S(2)}) async-start(s32[16,4,1]{1,2,0:T(1,128)} %bitcast.7), calls=%async_computation.1 | async-start | bytes 16384 | tf_op jit(solution)/shard_map/all_to_all | solution.py:88
  25.2 167.4 %all-gather.5.cloned.1.call-start = ((), (), s32[]{:S(2)}) async-start(), calls=%async_computation.3 | async-start | bytes 1179648 | tf_op jit(solution)/shard_map/all_gather | solution.py:97
  157.7 12.7 %copy-start.9 = (bf16[1024,6656]{1,0:T(8,128)(2,1)S(1)}, bf16[1024,6656]{1,0:T(8,128)(2,1)}, u32[]{:S(2)}) copy-start(bf16[1024,6656]{1,0:T(8,128)(2,1)} %all-gather.3.cloned.1.call-done) | copy-start | bytes 40894468
  157.7 23.3 %slice-start = ((s8[7340032]{0:T(1024)(128)(4,1)}), s8[4194304]{0:T(1024)(128)(4,1)S(1)}, s32[]{:S(2)}) async-start(s8[7340032]{0:T(1024)(128)(4,1)} %bitcast.26), calls=%async_computation.4 | async-start | bytes 8388608
  170.4 10.6 %slice-start.1 = ((s8[7340032]{0:T(1024)(128)(4,1)}), s8[3145728]{0:T(1024)(128)(4,1)S(1)}, s32[]{:S(2)}) async-start(s8[7340032]{0:T(1024)(128)(4,1)} %bitcast.26), calls=%async_computation.5 | async-start | bytes 6291456
  194.7 1.6 copy-start.2
  194.7 1.8 copy-start.10
  195.0 2.4 copy-start.13
  199.1 1.0 copy-start.3
  199.4 1.3 copy-start.4
  203.1 18.6 %copy-start.11 = (bf16[1024,512]{1,0:T(8,128)(2,1)S(1)}, bf16[1024,512]{1,0:T(8,128)(2,1)}, u32[]{:S(2)}) copy-start(bf16[1024,512]{1,0:T(8,128)(2,1)} %all-gather.5.cloned.1.call-done) | copy-start | bytes 3145732
  203.1 40.8 %all-to-all-start = ((bf16[64,2,16,4,128]{4,2,3,1,0:T(8,128)(2,1)}), bf16[64,2,16,4,128]{4,2,3,1,0:T(8,128)(2,1)S(1)}, u32[]{:S(2)}, u32[]{:S(2)}) async-start(bf16[64,2,16,4,128]{4,2,3,1,0:T(8,128)(2,1)} %gather_fusion), calls=%async_computation | async-start | bytes 4194304 | tf_op jit(solution)/shard_map/all_to_all | solution.py:90
Sparse Core Ops, SparseCore 0:
  13.3 144.3 all-gather.2
  160.0 32.5 all-gather.4
where the time goes:
time: 257 us; the launch traced here: 256 us
  waiting for transfers between devices  140 us (54%)
  matrix products  39 us (15%)
  starting transfers between devices  20.9 us (8%)
  local copies, waits for them, and re-layouts  20.4 us (8%)
  between operations  14.3 us (6%)
  Pallas kernels  12.3 us (5%)
  other arithmetic  8.87 us (3%)
    all_gather x2, waiting for transfers between devices, project_chunks(): part = lax.all_gather(normed_local[:, lo:hi], 'tp', axis=0, tiled=True)  134 us
    dot_general x6, matrix products, project_chunks(): term = jnp.dot(part, w[lo:hi], preferred_element_type=jnp.float32)  39 us
    all_to_all x1, starting transfers between devices, send_pages(): lax.all_to_all(stacked[order], 'req', split_axis=0, concat_axis=0, tiled=...  12.4 us
    pallas_call x1, Pallas kernels, attend(): pl.pallas_call(kernel, grid=(positions // block,), in_specs=[pl.BlockSpec...  12.3 us
    all_to_all x1, starting transfers between devices, send_pages(): lax.all_to_all(local_slot[order], 'req', split_axis=0, concat_axis=0, til...  8.44 us
    unnamed x33, local copies, waits for them, and re-layouts  6.72 us
    all_to_all x1, waiting for transfers between devices, send_pages(): lax.all_to_all(stacked[order], 'req', split_axis=0, concat_axis=0, tiled=...  6.41 us
  transfers between devices with their start and end apart: 4, of which 3 were waited for; matrix products, arithmetic and copies ran while one was open for 21% of the time, Pallas kernels for 5%

commit v1 on v0

--- a/solution.py
+++ b/solution.py
@@ -7,7 +7,6 @@
 from jax.sharding import PartitionSpec as P
 
 HEAD_DIM = 128
-SPLIT = 6656
 Q_BLOCK = 256
 
 
@@ -95,9 +94,9 @@
     sums = [None, None, None]
     for lo, hi in zip(bounds[:-1], bounds[1:]):
         part = lax.all_gather(normed_local[:, lo:hi], "tp", axis=0, tiled=True)
-        for i, w in enumerate((w_value, w_key, w_query)):
+        for i, w in enumerate((w_query, w_key, w_value)):
             term = jnp.dot(part, w[lo:hi], preferred_element_type=jnp.float32)
-            sums[2 - i] = term if sums[2 - i] is None else sums[2 - i] + term
+            sums[i] = term if sums[i] is None else sums[i] + term
         if hi < bounds[-1]:
             sums = list(lax.optimization_barrier(tuple(sums)))
     query = (sums[0] + qkv_bias[0]) * HEAD_DIM ** (-0.5)
@@ -109,7 +108,6 @@
 def on_device(
     hidden_in, ln_gain, ln_bias, w_query, w_key, w_value, qkv_bias, segment_ids, page_table
 ):
-    bounds = (0, SPLIT, hidden_in.shape[1])
     query, keys, values = project_chunks(
         layer_norm(hidden_in, ln_gain, ln_bias),
         w_query,
@@ -117,7 +115,7 @@
         w_value,
         qkv_bias,
         segment_ids >= 0,
-        bounds,
+        (0, hidden_in.shape[1]),
     )
     context = attend(query, keys, values, segment_ids)
     kv_cache = send_pages(keys, values, page_table)

time: 257 us -> 246 us (0.957)
  local copies, waits for them, and re-layouts: 20.4 us -> 15.1 us
  starting transfers between devices: 20.9 us -> 15.7 us
    all_to_all x1, starting transfers between devices: 12.4 us -> 7.26 us  [send_pages(): lax.all_to_all(stacked[order], 'req', split_axis=0, concat_axis=0, tiled=...]
    all_to_all x1, waiting for transfers between devices: 6.41 us -> 2.1 us  [send_pages(): lax.all_to_all(stacked[order], 'req', split_axis=0, concat_axis=0, tiled=...]
    all_to_all x1, waiting for transfers between devices: 0.01 us -> 4.08 us  [send_pages(): lax.all_to_all(local_slot[order], 'req', split_axis=0, concat_axis=0, til...]
    slice x3 -> x1, local copies, waits for them, and re-layouts: 2.96 us -> 0.07 us  [the longest x2 2.89 us: project_chunks(): part = lax.all_gather(normed_local[:, lo:hi], 'tp', axis=0, tiled=True)]
    unnamed x33 -> x19, local copies, waits for them, and re-layouts: 6.72 us -> 4.36 us
    all_gather x2 -> x1, waiting for transfers between devices: 134 us -> 132 us  [project_chunks(): part = lax.all_gather(normed_local[:, lo:hi], 'tp', axis=0, tiled=True)]
    dot_general x6 -> x3, matrix products: 39 us -> 40.3 us  [project_chunks(): term = jnp.dot(part, w[lo:hi], preferred_element_type=jnp.float32)]
  transfers between devices with their start and end apart: 4 -> 3, of which waited for: 3 -> 3; matrix products, arithmetic and copies ran while one was open for 21% -> 9% of each run, Pallas kernels for 5% -> 5%
where the time goes in v1:
time: 246 us
  waiting for transfers between devices  138 us (56%)
  matrix products  40.3 us (16%)
  starting transfers between devices  15.7 us (6%)
  local copies, waits for them, and re-layouts  15.1 us (6%)
  between operations  14.2 us (6%)
  Pallas kernels  12.3 us (5%)
  other arithmetic  10.1 us (4%)
    all_gather x1, waiting for transfers between devices, project_chunks(): part = lax.all_gather(normed_local[:, lo:hi], 'tp', axis=0, tiled=True)  132 us
    dot_general x3, matrix products, project_chunks(): term = jnp.dot(part, w[lo:hi], preferred_element_type=jnp.float32)  40.3 us
    pallas_call x1, Pallas kernels, attend(): pl.pallas_call(kernel, grid=(positions // block,), in_specs=[pl.BlockSpec...  12.3 us
    all_to_all x1, starting transfers between devices, send_pages(): lax.all_to_all(local_slot[order], 'req', split_axis=0, concat_axis=0, til...  8.44 us
    all_to_all x1, starting transfers between devices, send_pages(): lax.all_to_all(stacked[order], 'req', split_axis=0, concat_axis=0, tiled=...  7.26 us
  transfers between devices with their start and end apart: 3, of which 3 were waited for; matrix products, arithmetic and copies ran while one was open for 9% of the time, Pallas kernels for 5%

profile of v1, /device:TPU:1, one launch (start us, length us, event | category | flops | bytes accessed | tf_op | source)
XLA Modules:
  0.0 246.0 jit_solution(13481957364700510850)
XLA Ops:
  7.2 1.9 convert_reduce_fusion
  9.2 0.6 fusion.2
  9.9 2.0 fusion.5
  12.0 2.0 sort.34
  14.0 0.8 gather_fusion.1
  14.8 0.7 all_to_all.12
  15.5 8.4 %all-to-all-start.1 = ((s32[16,4,1]{1,2,0:T(1,128)}), s32[16,4,1]{1,2,0:T(1,128)S(1)}, u32[]{:S(2)}, u32[]{:S(2)}) async-start(s32[16,4,1]{1,2,0:T(1,128)} %bitcast.7), calls=%async_computation.1 | async-start | bytes 16384 | tf_op jit(solution)/shard_map/all_to_all | solution.py:87
  24.7 1.1 copy.19.lo_ref
  25.7 1.1 copy.20.hi_ref
  26.8 4.1 %all-to-all-done.1 = s32[16,4,1]{1,2,0:T(1,128)S(1)} async-done(((s32[16,4,1]{1,2,0:T(1,128)}), s32[16,4,1]{1,2,0:T(1,128)S(1)}, u32[]{:S(2)}, u32[]{:S(2)}) %all-to-all-start.1) | async-done | bytes 288 | tf_op jit(solution)/shard_map/all_to_all | solution.py:87
  31.4 0.7 reduce.5
  32.1 2.0 sort.35
  34.2 132.1 %all-gather.2.cloned.1.call-done = bf16[1024,7168]{1,0:T(8,128)(2,1)} async-done(((bf16[128,7168]{1,0:T(8,128)(2,1)}), bf16[1024,7168]{1,0:T(8,128)(2,1)}) %all-gather.2.cloned.1.call-update) | async-done | bytes 14680080 | tf_op jit(solution)/shard_map/all_gather | solution.py:96
  166.3 13.2 %select_convert_fusion.1.k_ref = bf16[1024,512]{1,0:T(8,128)(2,1)S(1)} fusion(bf16[1024,7168]{1,0:T(8,128)(2,1)} %all-gather.2.cloned.1.call-done, bf16[7168,512]{1,0:T(8,128)(2,1)} %param.13, f32[512]{0:T(512)S(1)} %bitcast.25, pred[1024]{0:T(1024)(128)(4,1)S(1)} %get-tuple-element.13), kind=kOutput, calls=%fused_computation.13 | convolution fusion | flops 7517765632 | bytes 23071744 | tf_op jit(solution)/shard_map/dot_general | solution.py:98
  179.8 1.2 copy.21
  181.0 13.2 %select_convert_fusion.v_ref = bf16[1024,512]{1,0:T(8,128)(2,1)S(1)} fusion(bf16[1024,7168]{1,0:T(8,128)(2,1)} %all-gather.2.cloned.1.call-done, bf16[7168,512]{1,0:T(8,128)(2,1)} %param.14, f32[512]{0:T(512)S(1)} %bitcast.24, pred[1024]{0:T(1024)(128)(4,1)S(1)} %get-tuple-element.13), kind=kOutput, calls=%fused_computation.12 | convolution fusion | flops 7517765632 | bytes 23071744 | tf_op jit(solution)/shard_map/dot_general | solution.py:98
  195.2 0.6 copy-done.3
  196.0 2.1 gather_fusion
  198.1 7.3 %all-to-all-start = ((bf16[64,2,16,4,128]{4,2,3,1,0:T(8,128)(2,1)}), bf16[64,2,16,4,128]{4,2,3,1,0:T(8,128)(2,1)S(1)}, u32[]{:S(2)}, u32[]{:S(2)}) async-start(bf16[64,2,16,4,128]{4,2,3,1,0:T(8,128)(2,1)} %gather_fusion), calls=%async_computation | async-start | bytes 4194304 | tf_op jit(solution)/shard_map/all_to_all | solution.py:89
  205.4 13.9 %multiply_convert_fusion.q_ref = bf16[1024,512]{1,0:T(8,128)(2,1)} fusion(bf16[1024,7168]{1,0:T(8,128)(2,1)} %all-gather.2.cloned.1.call-done, bf16[7168,512]{1,0:T(8,128)(2,1)} %param.12, f32[512]{0:T(512)S(1)} %bitcast.23), kind=kOutput, calls=%fused_computation.14 | convolution fusion | flops 7517765632 | bytes 23070720 | tf_op jit(solution)/shard_map/dot_general | solution.py:98
  219.3 12.3 %shard_map.104 = bf16[1024,512]{1,0:T(8,128)(2,1)} custom-call(bf16[1024,512]{1,0:T(8,128)(2,1)} %multiply_convert_fusion.q_ref, bf16[1024,512]{1,0:T(8,128)(2,1)} %copy-done.1, bf16[1024,512]{1,0:T(8,128)(2,1)} %copy-done.2, s32[1024,1]{1,0:T(8,128)} %copy.19.lo_ref, s32[1024,1]{1,0:T(8,128)} %copy.20.hi_ref), custom_call_target="tpu_custom_call" | custom-call | tf_op jit(solution)/shard_map/pallas_call | solution.py:59
  231.6 2.1 all-to-all-done
  233.7 2.2 gather_fusion.2
  235.9 3.3 %copy.24 = bf16[2,4,64,16,128]{4,3,2,1,0:T(8,128)(2,1)} copy(bf16[2,4,64,16,128]{4,3,1,0,2:T(8,128)(2,1)} %bitcast.20) | data formatting | bytes 4194304
  (43 shorter events, 2.9 us)
Async XLA Ops:
  7.2 2.1 copy-start
  7.2 2.7 %copy-start.6 = (f32[7168]{0:T(1024)S(1)}, f32[7168]{0:T(1024)}, u32[]{:S(2)}) copy-start(f32[7168]{0:T(1024)} %param.10) | copy-start | bytes 86020
  7.2 2.7 %copy-start.5 = (f32[7168]{0:T(1024)S(1)}, f32[7168]{0:T(1024)}, u32[]{:S(2)}) copy-start(f32[7168]{0:T(1024)} %param.11) | copy-start | bytes 86020
  7.2 159.1 %all-gather.2.cloned.1.call-start = ((), (), s32[]{:S(2)}) async-start(), calls=%async_computation.2 | async-start | bytes 16515072 | tf_op jit(solution)/shard_map/all_gather | solution.py:96
  9.9 2.0 copy-start.8
  11.9 12.0 %copy-start.4 = (s32[1024]{0:T(1024)S(1)}, s32[1024]{0:T(1024)}, u32[]{:S(2)}) copy-start(s32[1024]{0:T(1024)} %param.16) | copy-start | bytes 12292
  11.9 12.8 %copy-start.7 = (f32[3,512]{1,0:T(4,128)S(1)}, f32[3,512]{1,0:T(4,128)}, u32[]{:S(2)}) copy-start(f32[3,512]{1,0:T(4,128)} %param.15) | copy-start | bytes 18436
  15.5 15.4 %all-to-all-start.1 = ((s32[16,4,1]{1,2,0:T(1,128)}), s32[16,4,1]{1,2,0:T(1,128)S(1)}, u32[]{:S(2)}, u32[]{:S(2)}) async-start(s32[16,4,1]{1,2,0:T(1,128)} %bitcast.7), calls=%async_computation.1 | async-start | bytes 16384 | tf_op jit(solution)/shard_map/all_to_all | solution.py:87
  179.5 1.6 copy-start.1
  194.2 1.0 copy-start.2
  194.5 1.3 copy-start.3
  198.1 35.6 %all-to-all-start = ((bf16[64,2,16,4,128]{4,2,3,1,0:T(8,128)(2,1)}), bf16[64,2,16,4,128]{4,2,3,1,0:T(8,128)(2,1)S(1)}, u32[]{:S(2)}, u32[]{:S(2)}) async-start(bf16[64,2,16,4,128]{4,2,3,1,0:T(8,128)(2,1)} %gather_fusion), calls=%async_computation | async-start | bytes 4194304 | tf_op jit(solution)/shard_map/all_to_all | solution.py:89
Sparse Core Ops, SparseCore 0:
  12.0 154.1 all-gather.1

commit v2 on v1

--- a/solution.py
+++ b/solution.py
@@ -7,6 +7,7 @@
 from jax.sharding import PartitionSpec as P
 
 HEAD_DIM = 128
+LATE_ROWS = 16
 Q_BLOCK = 256
 
 
@@ -90,32 +91,63 @@
     return moved[inverse].transpose(1, 3, 0, 2, 4)
 
 
-def project_chunks(normed_local, w_query, w_key, w_value, qkv_bias, live, bounds):
-    sums = [None, None, None]
-    for lo, hi in zip(bounds[:-1], bounds[1:]):
-        part = lax.all_gather(normed_local[:, lo:hi], "tp", axis=0, tiled=True)
-        for i, w in enumerate((w_query, w_key, w_value)):
-            term = jnp.dot(part, w[lo:hi], preferred_element_type=jnp.float32)
-            sums[i] = term if sums[i] is None else sums[i] + term
-        if hi < bounds[-1]:
-            sums = list(lax.optimization_barrier(tuple(sums)))
-    query = (sums[0] + qkv_bias[0]) * HEAD_DIM ** (-0.5)
-    keys = jnp.where(live[:, None], sums[1] + qkv_bias[1], 0.0)
-    values = jnp.where(live[:, None], sums[2] + qkv_bias[2], 0.0)
-    return (query.astype(jnp.bfloat16), keys.astype(jnp.bfloat16), values.astype(jnp.bfloat16))
+def project_rows(normed, w_query, w_key, w_value, qkv_bias, live):
+    keys = jnp.where(
+        live[:, None],
+        jnp.dot(normed, w_key, preferred_element_type=jnp.float32) + qkv_bias[1],
+        0.0,
+    ).astype(jnp.bfloat16)
+    values = jnp.where(
+        live[:, None],
+        jnp.dot(normed, w_value, preferred_element_type=jnp.float32) + qkv_bias[2],
+        0.0,
+    ).astype(jnp.bfloat16)
+    query = (
+        (jnp.dot(normed, w_query, preferred_element_type=jnp.float32) + qkv_bias[0])
+        * HEAD_DIM ** (-0.5)
+    ).astype(jnp.bfloat16)
+    return [query, keys, values]
+
+
+def project_split(normed_local, w_query, w_key, w_value, qkv_bias, live):
+    rows = normed_local.shape[0]
+    early = rows - LATE_ROWS
+    parts = lax.axis_size("tp")
+    me = lax.axis_index("tp")
+    first = lax.all_gather(normed_local[:early], "tp", axis=0, tiled=True)
+    received = [normed_local[early:]] + [
+        lax.ppermute(
+            normed_local[early:], "tp", [(i, (i + s) % parts) for i in range(parts)]
+        )
+        for s in range(1, parts)
+    ]
+    late = jnp.take(jnp.stack(received), (me - jnp.arange(parts)) % parts, axis=0)
+    late = late.reshape(parts * LATE_ROWS, -1)
+    live_blocks = live.reshape(parts, rows)
+    early_out = project_rows(
+        first, w_query, w_key, w_value, qkv_bias, live_blocks[:, :early].reshape(-1)
+    )
+    late_out = project_rows(
+        late, w_query, w_key, w_value, qkv_bias, live_blocks[:, early:].reshape(-1)
+    )
+    return [
+        jnp.concatenate(
+            [a.reshape(parts, early, -1), b.reshape(parts, LATE_ROWS, -1)], axis=1
+        ).reshape(parts * rows, -1)
+        for a, b in zip(early_out, late_out)
+    ]
 
 
 def on_device(
     hidden_in, ln_gain, ln_bias, w_query, w_key, w_value, qkv_bias, segment_ids, page_table
 ):
-    query, keys, values = project_chunks(
+    query, keys, values = project_split(
         layer_norm(hidden_in, ln_gain, ln_bias),
         w_query,
         w_key,
         w_value,
         qkv_bias,
         segment_ids >= 0,
-        (0, hidden_in.shape[1]),
     )
     context = attend(query, keys, values, segment_ids)
     kv_cache = send_pages(keys, values, page_table)

time: 246 us -> 251 us (1.020)
  waiting for transfers between devices: 138 us -> 106 us
  starting transfers between devices: 15.7 us -> 33 us
  local copies, waits for them, and re-layouts: 15.1 us -> 25.9 us
  matrix products: 40.3 us -> 45.6 us
  other arithmetic: 10.1 us -> 13.3 us
    all_gather x1, waiting for transfers between devices: 132 us -> 72.9 us  [project_split(): first = lax.all_gather(normed_local[:early], 'tp', axis=0, tiled=True)]
    ppermute x0 -> x7, waiting for transfers between devices: none -> 21.6 us  [project_split(): lax.ppermute(normed_local[early:], 'tp', [(i, (i + s) % parts) for i in r...]
    ppermute x0 -> x7, starting transfers between devices: none -> 15.8 us  [project_split(): lax.ppermute(normed_local[early:], 'tp', [(i, (i + s) % parts) for i in r...]
    all_to_all x1, waiting for transfers between devices: 4.08 us -> 11.2 us  [send_pages(): lax.all_to_all(local_slot[order], 'req', split_axis=0, concat_axis=0, til...]
    dot_general x3 -> x6, matrix products: 40.3 us -> 45.6 us  [the longest x2 16.4 us: project_rows(): jnp.dot(normed, w_value, preferred_element_type=jnp.float32) + qkv_bias[2]]
    another operation x4, local copies, waits for them, and re-layouts: 2.08 us -> 6.62 us  [send_pages(): jnp.stack([keys, values], axis=0)]
  transfers between devices with their start and end apart: 3 -> 10, of which waited for: 3 -> 4; matrix products, arithmetic and copies ran while one was open for 9% -> 15% of each run, Pallas kernels for 5% -> 5%
where the time goes in v2:
time: 251 us; the launch traced here: 250 us
  waiting for transfers between devices  106 us (42%)
  matrix products  45.6 us (18%)
  starting transfers between devices  33 us (13%)
  local copies, waits for them, and re-layouts  25.9 us (10%)
  between operations  14.4 us (6%)
  other arithmetic  13.3 us (5%)
  Pallas kernels  12.3 us (5%)
    all_gather x1, waiting for transfers between devices, project_split(): first = lax.all_gather(normed_local[:early], 'tp', axis=0, tiled=True)  72.9 us
    ppermute x7, waiting for transfers between devices, project_split(): lax.ppermute(normed_local[early:], 'tp', [(i, (i + s) % parts) for i in r...  21.6 us
    dot_general x2, matrix products, project_rows(): jnp.dot(normed, w_value, preferred_element_type=jnp.float32) + qkv_bias[2]  16.4 us
    dot_general x2, matrix products, project_rows(): jnp.dot(normed, w_query, preferred_element_type=jnp.float32) + qkv_bias[0]  16.1 us
    ppermute x7, starting transfers between devices, project_split(): lax.ppermute(normed_local[early:], 'tp', [(i, (i + s) % parts) for i in r...  15.8 us
    dot_general x2, matrix products, project_rows(): jnp.dot(normed, w_key, preferred_element_type=jnp.float32) + qkv_bias[1]  13.1 us
    pallas_call x1, Pallas kernels, attend(): pl.pallas_call(kernel, grid=(positions // block,), in_specs=[pl.BlockSpec...  12.3 us
    all_to_all x1, waiting for transfers between devices, send_pages(): lax.all_to_all(local_slot[order], 'req', split_axis=0, concat_axis=0, til...  11.2 us
  transfers between devices with their start and end apart: 10, of which 4 were waited for; matrix products, arithmetic and copies ran while one was open for 15% of the time, Pallas kernels for 5%

profile of v2, /device:TPU:1, one launch (start us, length us, event | category | flops | bytes accessed | tf_op | source)
XLA Modules:
  0.0 250.2 jit_solution(9148136349453705021)
XLA Ops:
  7.2 1.9 convert_reduce_fusion
  14.2 5.4 %collective-permute-start.5 = (bf16[16,7168]{1,0:T(8,128)(2,1)S(1)}, bf16[16,7168]{1,0:T(8,128)(2,1)S(1)}, u32[]{:S(2)}, u32[]{:S(2)}) collective-permute-start(bf16[16,7168]{1,0:T(8,128)(2,1)S(1)} %slice.64), channel_id=1, source_target_pairs={{0,6},{1,7},{2,0},{3,1},{4,2},{5,3},{6,4},{7,5},{8,14},{9,15},{10,... | collective-permute-start | bytes 688136 | tf_op jit(solution)/shard_map/ppermute | solution.py:119
  23.0 2.0 sort.34
  26.5 9.0 %all-to-all-start.1 = ((s32[16,4,1]{1,2,0:T(1,128)}), s32[16,4,1]{1,2,0:T(1,128)S(1)}, u32[]{:S(2)}, u32[]{:S(2)}) async-start(s32[16,4,1]{1,2,0:T(1,128)} %bitcast.27), calls=%async_computation.1 | async-start | bytes 16384 | tf_op jit(solution)/shard_map/all_to_all | solution.py:88
  39.8 11.2 %all-to-all-done.1 = s32[16,4,1]{1,2,0:T(1,128)S(1)} async-done(((s32[16,4,1]{1,2,0:T(1,128)}), s32[16,4,1]{1,2,0:T(1,128)S(1)}, u32[]{:S(2)}, u32[]{:S(2)}) %all-to-all-start.1) | async-done | bytes 288 | tf_op jit(solution)/shard_map/all_to_all | solution.py:88
  52.3 2.0 sort.35
  54.4 11.9 %collective-permute-done.1 = bf16[16,7168]{1,0:T(8,128)(2,1)S(1)} collective-permute-done((bf16[16,7168]{1,0:T(8,128)(2,1)S(1)}, bf16[16,7168]{1,0:T(8,128)(2,1)S(1)}, u32[]{:S(2)}, u32[]{:S(2)}) %collective-permute-start.1) | collective-permute-done | bytes 229408 | tf_op jit(solution)/shard_map/ppermute | solution.py:119
  66.3 7.0 %collective-permute-start.6 = (bf16[16,7168]{1,0:T(8,128)(2,1)S(1)}, bf16[16,7168]{1,0:T(8,128)(2,1)S(1)}, u32[]{:S(2)}, u32[]{:S(2)}) collective-permute-start(bf16[16,7168]{1,0:T(8,128)(2,1)S(1)} %slice.64), channel_id=1, source_target_pairs={{0,7},{1,0},{2,1},{3,2},{4,3},{5,4},{6,5},{7,6},{8,15},{9,8},{10,9... | collective-permute-start | bytes 688136 | tf_op jit(solution)/shard_map/ppermute | solution.py:119
  73.5 9.7 %collective-permute-done.6 = bf16[16,7168]{1,0:T(8,128)(2,1)S(1)} collective-permute-done((bf16[16,7168]{1,0:T(8,128)(2,1)S(1)}, bf16[16,7168]{1,0:T(8,128)(2,1)S(1)}, u32[]{:S(2)}, u32[]{:S(2)}) %collective-permute-start.6) | collective-permute-done | bytes 229408 | tf_op jit(solution)/shard_map/ppermute | solution.py:119
  83.2 1.9 gather_fusion
  85.1 1.9 bitcast_select_fusion
  87.0 4.5 %fusion.11 = bf16[128,512]{1,0:T(8,128)(2,1)S(1)} fusion(bf16[128,7168]{1,0:T(8,128)(2,1)S(1)} %bitcast_select_fusion, bf16[7168,512]{1,0:T(8,128)(2,1)} %param.14, f32[512]{0:T(512)S(1)} %bitcast.75, pred[128]{0:T(512)(128)(4,1)S(1)} %broadcast_in_dim.73), kind=kOutput, calls=%fused_computation.25 | convolution fusion | flops 939720704 | bytes 9308288 | tf_op jit(solution)/shard_map/dot_general | solution.py:102
  92.7 72.9 %all-gather.2.cloned.1.call-done = bf16[896,7168]{1,0:T(8,128)(2,1)} async-done(((bf16[112,7168]{1,0:T(8,128)(2,1)}), bf16[896,7168]{1,0:T(8,128)(2,1)}) %all-gather.2.cloned.1.call-update) | async-done | bytes 12845072 | tf_op jit(solution)/shard_map/all_gather | solution.py:117
  165.5 12.0 %select_convert_fusion.1 = bf16[896,512]{1,0:T(8,128)(2,1)S(1)} fusion(bf16[896,7168]{1,0:T(8,128)(2,1)} %all-gather.2.cloned.1.call-done, bf16[7168,512]{1,0:T(8,128)(2,1)} %param.13, f32[512]{0:T(512)S(1)} %bitcast.78, pred[896]{0:T(1024)(128)(4,1)S(1)} %broadcast_in_dim.70), kind=kOutput, calls=%fused_computation.15 | convolution fusion | flops 6578044928 | bytes 21105536 | tf_op jit(solution)/shard_map/dot_general | solution.py:97
  178.9 2.5 copy.24
  181.3 12.0 %select_convert_fusion = bf16[896,512]{1,0:T(8,128)(2,1)S(1)} fusion(bf16[896,7168]{1,0:T(8,128)(2,1)} %all-gather.2.cloned.1.call-done, bf16[7168,512]{1,0:T(8,128)(2,1)} %param.14, f32[512]{0:T(512)S(1)} %bitcast.76, pred[896]{0:T(1024)(128)(4,1)S(1)} %broadcast_in_dim.70), kind=kOutput, calls=%fused_computation.14 | convolution fusion | flops 6578044928 | bytes 21105536 | tf_op jit(solution)/shard_map/dot_general | solution.py:102
  194.7 1.6 copy.25
  197.8 3.7 %gather_fusion.1 = bf16[64,2,16,4,128]{4,2,3,1,0:T(8,128)(2,1)} fusion(bf16[64,2,16,4,128]{4,2,3,1,0:T(8,128)(2,1)} %maximum_bitcast_fusion, s32[1024]{0:T(1024)S(1)} %pad_clamp_fusion.1), kind=kCustom, calls=%fused_computation.1 | custom fusion | bytes 4194560 | tf_op jit(solution)/shard_map/gather | solution.py:90
  201.5 8.1 %all-to-all-start = ((bf16[64,2,16,4,128]{4,2,3,1,0:T(8,128)(2,1)}), bf16[64,2,16,4,128]{4,2,3,1,0:T(8,128)(2,1)}, u32[]{:S(2)}, u32[]{:S(2)}) async-start(bf16[64,2,16,4,128]{4,2,3,1,0:T(8,128)(2,1)} %gather_fusion.1), calls=%async_computation | async-start | bytes 4194304 | tf_op jit(solution)/shard_map/all_to_all | solution.py:90
  209.6 4.2 %fusion.9 = bf16[128,512]{1,0:T(8,128)(2,1)S(1)} fusion(bf16[128,7168]{1,0:T(8,128)(2,1)S(1)} %bitcast_select_fusion, bf16[7168,512]{1,0:T(8,128)(2,1)} %param.12, f32[512]{0:T(512)S(1)} %bitcast.73), kind=kOutput, calls=%fused_computation.23 | convolution fusion | flops 939720704 | bytes 9308160 | tf_op jit(solution)/shard_map/dot_general | solution.py:106
  213.8 11.9 %multiply_convert_fusion = bf16[896,512]{1,0:T(8,128)(2,1)S(1)} fusion(bf16[896,7168]{1,0:T(8,128)(2,1)} %all-gather.2.cloned.1.call-done, bf16[7168,512]{1,0:T(8,128)(2,1)} %param.12, f32[512]{0:T(512)S(1)} %bitcast.74), kind=kOutput, calls=%fused_computation.16 | convolution fusion | flops 6578044928 | bytes 21104640 | tf_op jit(solution)/shard_map/dot_general | solution.py:106
  226.7 12.3 %shard_map.104 = bf16[1024,512]{1,0:T(8,128)(2,1)} custom-call(bf16[1024,512]{1,0:T(8,128)(2,1)} %bitcast.62, bf16[1024,512]{1,0:T(8,128)(2,1)} %bitcast.59, bf16[1024,512]{1,0:T(8,128)(2,1)} %bitcast.60, s32[1024,1]{1,0:T(8,128)} %copy.22.lo_ref, s32[1024,1]{1,0:T(8,128)} %copy.23.hi_ref), custom_call_target="tpu_custom_call" | custom-call | tf_op jit(solution)/shard_map/pallas_call | solution.py:60
  239.1 2.5 %gather_fusion.3 = bf16[64,2,16,4,128]{4,2,3,1,0:T(8,128)(2,1)S(1)} fusion(bf16[64,2,16,4,128]{4,2,3,1,0:T(8,128)(2,1)} %all-to-all-done, s32[1024]{0:T(1024)S(1)} %pad_clamp_fusion), kind=kCustom, calls=%fused_computation.3 | custom fusion | bytes 4194560 | tf_op jit(solution)/shard_map/gather | solution.py:91
  241.6 1.7 copy.27
  (90 shorter events, 22.0 us)
Async XLA Ops:
  7.2 2.1 copy-start
  7.2 2.7 %copy-start.6 = (f32[7168]{0:T(1024)S(1)}, f32[7168]{0:T(1024)}, u32[]{:S(2)}) copy-start(f32[7168]{0:T(1024)} %param.11) | copy-start | bytes 86020
  7.2 2.7 %copy-start.7 = (f32[7168]{0:T(1024)S(1)}, f32[7168]{0:T(1024)}, u32[]{:S(2)}) copy-start(f32[7168]{0:T(1024)} %param.10) | copy-start | bytes 86020
  7.2 158.3 %all-gather.2.cloned.1.call-start = ((), (), s32[]{:S(2)}) async-start(), calls=%async_computation.2 | async-start | bytes 14450688 | tf_op jit(solution)/shard_map/all_gather | solution.py:117
  10.7 1.2 copy-start.3
  11.9 11.1 %copy-start.9 = (s32[64]{0:T(128)S(1)}, s32[64]{0:T(128)}, u32[]{:S(2)}) copy-start(s32[64]{0:T(128)} %param.17) | copy-start | bytes 772
  13.2 22.5 %copy-start.5 = (s32[1024]{0:T(1024)S(1)}, s32[1024]{0:T(1024)}, u32[]{:S(2)}) copy-start(s32[1024]{0:T(1024)} %param.16) | copy-start | bytes 12292
  13.2 23.5 %copy-start.8 = (f32[3,512]{1,0:T(4,128)S(1)}, f32[3,512]{1,0:T(4,128)}, u32[]{:S(2)}) copy-start(f32[3,512]{1,0:T(4,128)} %param.15) | copy-start | bytes 18436
  14.2 59.3 %collective-permute-start.5 = (bf16[16,7168]{1,0:T(8,128)(2,1)S(1)}, bf16[16,7168]{1,0:T(8,128)(2,1)S(1)}, u32[]{:S(2)}, u32[]{:S(2)}) collective-permute-start(bf16[16,7168]{1,0:T(8,128)(2,1)S(1)} %slice.64), channel_id=1, source_target_pairs={{0,6},{1,7},{2,0},{3,1},{4,2},{5,3},{6,4},{7,5},{8,14},{9,15},{10,... | collective-permute-start | bytes 688136 | tf_op jit(solution)/shard_map/ppermute | solution.py:119
  19.6 53.8 %collective-permute-start.4 = (bf16[16,7168]{1,0:T(8,128)(2,1)S(1)}, bf16[16,7168]{1,0:T(8,128)(2,1)S(1)}, u32[]{:S(2)}, u32[]{:S(2)}) collective-permute-start(bf16[16,7168]{1,0:T(8,128)(2,1)S(1)} %slice.64), channel_id=1, source_target_pairs={{0,5},{1,6},{2,7},{3,0},{4,1},{5,2},{6,3},{7,4},{8,13},{9,14},{10,... | collective-permute-start | bytes 688136 | tf_op jit(solution)/shard_map/ppermute | solution.py:119
  20.3 53.1 %collective-permute-start.3 = (bf16[16,7168]{1,0:T(8,128)(2,1)S(1)}, bf16[16,7168]{1,0:T(8,128)(2,1)S(1)}, u32[]{:S(2)}, u32[]{:S(2)}) collective-permute-start(bf16[16,7168]{1,0:T(8,128)(2,1)S(1)} %slice.64), channel_id=1, source_target_pairs={{0,4},{1,5},{2,6},{3,7},{4,0},{5,1},{6,2},{7,3},{8,12},{9,13},{10,... | collective-permute-start | bytes 688136 | tf_op jit(solution)/shard_map/ppermute | solution.py:119
  21.5 51.8 %collective-permute-start.2 = (bf16[16,7168]{1,0:T(8,128)(2,1)S(1)}, bf16[16,7168]{1,0:T(8,128)(2,1)S(1)}, u32[]{:S(2)}, u32[]{:S(2)}) collective-permute-start(bf16[16,7168]{1,0:T(8,128)(2,1)S(1)} %slice.64), channel_id=1, source_target_pairs={{0,3},{1,4},{2,5},{3,6},{4,7},{5,0},{6,1},{7,2},{8,11},{9,12},{10,... | collective-permute-start | bytes 688136 | tf_op jit(solution)/shard_map/ppermute | solution.py:119
  22.5 31.8 %collective-permute-start = (bf16[16,7168]{1,0:T(8,128)(2,1)S(1)}, bf16[16,7168]{1,0:T(8,128)(2,1)S(1)}, u32[]{:S(2)}, u32[]{:S(2)}) collective-permute-start(bf16[16,7168]{1,0:T(8,128)(2,1)S(1)} %slice.64), channel_id=1, source_target_pairs={{0,1},{1,2},{2,3},{3,4},{4,5},{5,6},{6,7},{7,0},{8,9},{9,10},{10,1... | collective-permute-start | bytes 688136 | tf_op jit(solution)/shard_map/ppermute | solution.py:119
  26.5 24.5 %all-to-all-start.1 = ((s32[16,4,1]{1,2,0:T(1,128)}), s32[16,4,1]{1,2,0:T(1,128)S(1)}, u32[]{:S(2)}, u32[]{:S(2)}) async-start(s32[16,4,1]{1,2,0:T(1,128)} %bitcast.27), calls=%async_computation.1 | async-start | bytes 16384 | tf_op jit(solution)/shard_map/all_to_all | solution.py:88
  54.3 12.0 %collective-permute-start.1 = (bf16[16,7168]{1,0:T(8,128)(2,1)S(1)}, bf16[16,7168]{1,0:T(8,128)(2,1)S(1)}, u32[]{:S(2)}, u32[]{:S(2)}) collective-permute-start(bf16[16,7168]{1,0:T(8,128)(2,1)S(1)} %slice.64), channel_id=1, source_target_pairs={{0,2},{1,3},{2,4},{3,5},{4,6},{5,7},{6,0},{7,1},{8,10},{9,11},{10,... | collective-permute-start | bytes 688136 | tf_op jit(solution)/shard_map/ppermute | solution.py:119
  66.3 16.9 %collective-permute-start.6 = (bf16[16,7168]{1,0:T(8,128)(2,1)S(1)}, bf16[16,7168]{1,0:T(8,128)(2,1)S(1)}, u32[]{:S(2)}, u32[]{:S(2)}) collective-permute-start(bf16[16,7168]{1,0:T(8,128)(2,1)S(1)} %slice.64), channel_id=1, source_target_pairs={{0,7},{1,0},{2,1},{3,2},{4,3},{5,4},{6,5},{7,6},{8,15},{9,8},{10,9... | collective-permute-start | bytes 688136 | tf_op jit(solution)/shard_map/ppermute | solution.py:119
  85.1 6.4 %slice-start = ((s8[7340032]{0:T(1024)(128)(4,1)}), s8[4194304]{0:T(1024)(128)(4,1)S(1)}, s32[]{:S(2)}) async-start(s8[7340032]{0:T(1024)(128)(4,1)} %bitcast.57), calls=%async_computation.3 | async-start | bytes 8388608
  87.0 4.5 %slice-start.1 = ((s8[7340032]{0:T(1024)(128)(4,1)}), s8[3145728]{0:T(1024)(128)(4,1)S(1)}, s32[]{:S(2)}) async-start(s8[7340032]{0:T(1024)(128)(4,1)} %bitcast.57), calls=%async_computation.4 | async-start | bytes 6291456
  177.6 3.8 %copy-start.1 = (bf16[8,128,512]{2,1,0:T(8,128)(2,1)}, bf16[8,128,512]{2,1,0:T(8,128)(2,1)S(1)}, u32[]{:S(2)}) copy-start(bf16[8,128,512]{2,1,0:T(8,128)(2,1)S(1)} %pad_maximum_fusion.1) | copy-start | bytes 3145732
  193.4 2.9 %copy-start.2 = (bf16[8,128,512]{2,1,0:T(8,128)(2,1)}, bf16[8,128,512]{2,1,0:T(8,128)(2,1)S(1)}, u32[]{:S(2)}) copy-start(bf16[8,128,512]{2,1,0:T(8,128)(2,1)S(1)} %pad_maximum_fusion.2) | copy-start | bytes 3145732
  194.7 1.6 copy-start.4
  201.5 37.6 %all-to-all-start = ((bf16[64,2,16,4,128]{4,2,3,1,0:T(8,128)(2,1)}), bf16[64,2,16,4,128]{4,2,3,1,0:T(8,128)(2,1)}, u32[]{:S(2)}, u32[]{:S(2)}) async-start(bf16[64,2,16,4,128]{4,2,3,1,0:T(8,128)(2,1)} %gather_fusion.1), calls=%async_computation | async-start | bytes 4194304 | tf_op jit(solution)/shard_map/all_to_all | solution.py:90
Sparse Core Ops, SparseCore 0:
  13.3 152.1 all-gather.1

commit v3 on v1

--- a/solution.py
+++ b/solution.py
@@ -48,7 +48,7 @@
                 ).astype(o_ref.dtype)
 
 
-def attend(query, keys, values, segments):
+def attend(query, kv, segments):
     positions, width = query.shape
     block = Q_BLOCK
     position = jnp.arange(positions, dtype=jnp.int32)
@@ -62,25 +62,21 @@
         in_specs=[
             pl.BlockSpec((block, width), lambda i: (i, 0)),
             pl.BlockSpec((positions, width), lambda i: (0, 0)),
-            pl.BlockSpec((positions, width), lambda i: (0, 0)),
+            pl.BlockSpec((positions, width), lambda i: (0, 1)),
             pl.BlockSpec((block, 1), lambda i: (i, 0)),
             pl.BlockSpec((block, 1), lambda i: (i, 0)),
         ],
         out_specs=pl.BlockSpec((block, width), lambda i: (i, 0)),
         out_shape=jax.ShapeDtypeStruct((positions, width), query.dtype),
-    )(query, keys, values, lo.reshape(positions, 1), hi.reshape(positions, 1))
+    )(query, kv, kv, lo.reshape(positions, 1), hi.reshape(positions, 1))
 
 
-def send_pages(keys, values, page_table):
+def send_pages(kv, page_table):
     pages = page_table.shape[0]
-    positions, width = keys.shape
+    positions, width = kv.shape
     page_rows = positions // pages
-    heads = width // HEAD_DIM
-    stacked = (
-        jnp.stack([keys, values], axis=0)
-        .reshape(2, pages, page_rows, heads, HEAD_DIM)
-        .transpose(1, 0, 2, 3, 4)
-    )
+    heads = width // (2 * HEAD_DIM)
+    stacked = kv.reshape(pages, page_rows, 2, heads, HEAD_DIM).transpose(0, 2, 1, 3, 4)
     target = page_table // pages
     local_slot = page_table % pages
     order = jnp.argsort(target, stable=True)
@@ -90,35 +86,33 @@
     return moved[inverse].transpose(1, 3, 0, 2, 4)
 
 
-def project_chunks(normed_local, w_query, w_key, w_value, qkv_bias, live, bounds):
-    sums = [None, None, None]
-    for lo, hi in zip(bounds[:-1], bounds[1:]):
-        part = lax.all_gather(normed_local[:, lo:hi], "tp", axis=0, tiled=True)
-        for i, w in enumerate((w_query, w_key, w_value)):
-            term = jnp.dot(part, w[lo:hi], preferred_element_type=jnp.float32)
-            sums[i] = term if sums[i] is None else sums[i] + term
-        if hi < bounds[-1]:
-            sums = list(lax.optimization_barrier(tuple(sums)))
-    query = (sums[0] + qkv_bias[0]) * HEAD_DIM ** (-0.5)
-    keys = jnp.where(live[:, None], sums[1] + qkv_bias[1], 0.0)
-    values = jnp.where(live[:, None], sums[2] + qkv_bias[2], 0.0)
-    return (query.astype(jnp.bfloat16), keys.astype(jnp.bfloat16), values.astype(jnp.bfloat16))
+def project_all(normed_local, w_query, w_key, w_value, qkv_bias, live):
+    w_kv = jnp.concatenate([w_key, w_value], axis=1)
+    normed = lax.all_gather(normed_local, "tp", axis=0, tiled=True)
+    bias_kv = jnp.concatenate([qkv_bias[1], qkv_bias[2]])
+    kv = jnp.where(
+        live[:, None], jnp.dot(normed, w_kv, preferred_element_type=jnp.float32) + bias_kv, 0.0
+    ).astype(jnp.bfloat16)
+    query = (
+        (jnp.dot(normed, w_query, preferred_element_type=jnp.float32) + qkv_bias[0])
+        * HEAD_DIM ** (-0.5)
+    ).astype(jnp.bfloat16)
+    return (query, kv)
 
 
 def on_device(
     hidden_in, ln_gain, ln_bias, w_query, w_key, w_value, qkv_bias, segment_ids, page_table
 ):
-    query, keys, values = project_chunks(
+    query, kv = project_all(
         layer_norm(hidden_in, ln_gain, ln_bias),
         w_query,
         w_key,
         w_value,
         qkv_bias,
         segment_ids >= 0,
-        (0, hidden_in.shape[1]),
     )
-    context = attend(query, keys, values, segment_ids)
-    kv_cache = send_pages(keys, values, page_table)
+    context = attend(query, kv, segment_ids)
+    kv_cache = send_pages(kv, page_table)
     return (context, kv_cache)
 
 

time: 246 us -> 249 us (1.012)
  local copies, waits for them, and re-layouts: 15.1 us -> 20.2 us
  matrix products: 40.3 us -> 36.4 us
    reshape x0 -> x2, local copies, waits for them, and re-layouts: none -> 6.66 us  [send_pages(): kv.reshape(pages, page_rows, 2, heads, HEAD_DIM).transpose(0, 2, 1, 3, 4)]
    dot_general x3 -> x2, matrix products: 40.3 us -> 36.4 us  [the longest x1 22.5 us: project_all(): jnp.dot(normed, w_kv, preferred_element_type=jnp.float32) + bias_kv]
where the time goes in v3:
time: 249 us
  waiting for transfers between devices  138 us (55%)
  matrix products  36.4 us (15%)
  local copies, waits for them, and re-layouts  20.2 us (8%)
  starting transfers between devices  15.7 us (6%)
  between operations  14.2 us (6%)
  Pallas kernels  12.3 us (5%)
  other arithmetic  11.4 us (5%)
    all_gather x1, waiting for transfers between devices, project_all(): normed = lax.all_gather(normed_local, 'tp', axis=0, tiled=True)  132 us
    dot_general x1, matrix products, project_all(): jnp.dot(normed, w_kv, preferred_element_type=jnp.float32) + bias_kv  22.5 us
    dot_general x1, matrix products, project_all(): jnp.dot(normed, w_query, preferred_element_type=jnp.float32) + qkv_bias[0]  13.9 us
    pallas_call x1, Pallas kernels, attend(): pl.pallas_call(kernel, grid=(positions // block,), in_specs=[pl.BlockSpec...  12.3 us
    all_to_all x1, starting transfers between devices, send_pages(): lax.all_to_all(local_slot[order], 'req', split_axis=0, concat_axis=0, til...  8.44 us
    all_to_all x1, starting transfers between devices, send_pages(): lax.all_to_all(stacked[order], 'req', split_axis=0, concat_axis=0, tiled=...  7.27 us
    reshape x2, local copies, waits for them, and re-layouts, send_pages(): kv.reshape(pages, page_rows, 2, heads, HEAD_DIM).transpose(0, 2, 1, 3, 4)  6.66 us
  transfers between devices with their start and end apart: 3, of which 3 were waited for; matrix products, arithmetic and copies ran while one was open for 9% of the time, Pallas kernels for 5%

profile of v3, /device:TPU:1, one launch (start us, length us, event | category | flops | bytes accessed | tf_op | source)
XLA Modules:
  0.0 248.6 jit_solution(14038178452304593111)
XLA Ops:
  7.2 1.9 convert_reduce_fusion
  9.2 2.2 fusion.6
  11.4 2.0 fusion.9
  13.5 2.0 sort.34
  15.5 0.8 gather_fusion.1
  16.3 0.7 all_to_all.12
  17.0 8.4 %all-to-all-start.1 = ((s32[16,4,1]{1,2,0:T(1,128)}), s32[16,4,1]{1,2,0:T(1,128)S(1)}, u32[]{:S(2)}, u32[]{:S(2)}) async-start(s32[16,4,1]{1,2,0:T(1,128)} %bitcast.7), calls=%async_computation.1 | async-start | bytes 16384 | tf_op jit(solution)/shard_map/all_to_all | solution.py:83
  26.2 1.0 copy.18.lo_ref
  27.2 1.0 copy.19.hi_ref
  28.3 4.1 %all-to-all-done.1 = s32[16,4,1]{1,2,0:T(1,128)S(1)} async-done(((s32[16,4,1]{1,2,0:T(1,128)}), s32[16,4,1]{1,2,0:T(1,128)S(1)}, u32[]{:S(2)}, u32[]{:S(2)}) %all-to-all-start.1) | async-done | bytes 288 | tf_op jit(solution)/shard_map/all_to_all | solution.py:83
  32.4 0.5 broadcast.88
  32.9 0.7 reduce.5
  33.7 2.0 sort.35
  35.7 132.1 %all-gather.2.cloned.1.call-done = bf16[1024,7168]{1,0:T(8,128)(2,1)} async-done(((bf16[128,7168]{1,0:T(8,128)(2,1)}), bf16[1024,7168]{1,0:T(8,128)(2,1)}) %all-gather.2.cloned.1.call-update) | async-done | bytes 14680080 | tf_op jit(solution)/shard_map/all_gather | solution.py:91
  167.8 22.5 %select_convert_fusion.k_ref.v_ref = bf16[1024,1024]{1,0:T(8,128)(2,1)S(1)} fusion(f32[1024]{0:T(1024)S(1)} %pad_maximum_fusion, pred[1024]{0:T(1024)(128)(4,1)S(1)} %get-tuple-element.13, bf16[1024,7168]{1,0:T(8,128)(2,1)} %all-gather.2.cloned.1.call-done, bf16[7168,512]{1,0:T(8,128)(2,1)} %param.14, bf16[7168,512]{1,0:T(8,128)(2,1)} %param.13), kind=kOutput, calls=%fused_computation.11 | convolution fusion | flops 15064891392 | bytes 31462400 | tf_op jit(solution)/shard_map/dot_general | solution.py:94
  190.3 3.0 %reshape.64 = bf16[64,16,2,4,128]{4,3,2,1,0:T(4,128)(2,1)} reshape(bf16[1024,1024]{1,0:T(8,128)(2,1)S(1)} %select_convert_fusion.k_ref.v_ref) | data formatting | bytes 4194304 | tf_op jit(solution)/shard_map/reshape | solution.py:79
  193.3 3.6 %copy.24 = bf16[64,16,2,4,128]{4,1,3,2,0:T(8,128)(2,1)} copy(bf16[64,16,2,4,128]{4,3,2,1,0:T(4,128)(2,1)} %reshape.64) | data formatting | bytes 4194304 | tf_op jit(solution)/shard_map/reshape | solution.py:79
  197.0 3.7 %gather_fusion = bf16[64,2,16,4,128]{4,2,3,1,0:T(8,128)(2,1)} fusion(bf16[64,2,16,4,128]{4,2,3,1,0:T(8,128)(2,1)} %bitcast.18, s32[1024]{0:T(1024)S(1)} %pad_clamp_fusion.1), kind=kCustom, calls=%fused_computation | custom fusion | bytes 4194560 | tf_op jit(solution)/shard_map/gather | solution.py:85
  200.7 7.3 %all-to-all-start = ((bf16[64,2,16,4,128]{4,2,3,1,0:T(8,128)(2,1)}), bf16[64,2,16,4,128]{4,2,3,1,0:T(8,128)(2,1)S(1)}, u32[]{:S(2)}, u32[]{:S(2)}) async-start(bf16[64,2,16,4,128]{4,2,3,1,0:T(8,128)(2,1)} %gather_fusion), calls=%async_computation | async-start | bytes 4194304 | tf_op jit(solution)/shard_map/all_to_all | solution.py:85
  208.0 13.9 %multiply_convert_fusion.q_ref = bf16[1024,512]{1,0:T(8,128)(2,1)} fusion(bf16[1024,7168]{1,0:T(8,128)(2,1)} %all-gather.2.cloned.1.call-done, bf16[7168,512]{1,0:T(8,128)(2,1)} %param.12, f32[512]{0:T(512)S(1)} %bitcast.24), kind=kOutput, calls=%fused_computation.17 | convolution fusion | flops 7517765632 | bytes 23070720 | tf_op jit(solution)/shard_map/dot_general | solution.py:97
  221.9 12.3 %shard_map.104 = bf16[1024,512]{1,0:T(8,128)(2,1)} custom-call(bf16[1024,512]{1,0:T(8,128)(2,1)} %multiply_convert_fusion.q_ref, bf16[1024,1024]{1,0:T(8,128)(2,1)} %copy-done, bf16[1024,1024]{1,0:T(8,128)(2,1)} %copy-done, s32[1024,1]{1,0:T(8,128)} %copy.18.lo_ref, s32[1024,1]{1,0:T(8,128)} %copy.19.hi_ref), custom_call_target="tpu_custom_call" | custom-call | tf_op jit(solution)/shard_map/pallas_call | solution.py:59
  234.2 2.1 all-to-all-done
  236.3 2.2 gather_fusion.2
  238.5 3.3 %copy.22 = bf16[2,4,64,16,128]{4,3,2,1,0:T(8,128)(2,1)} copy(bf16[2,4,64,16,128]{4,3,1,0,2:T(8,128)(2,1)} %bitcast.19) | data formatting | bytes 4194304
  (36 shorter events, 1.0 us)
Async XLA Ops:
  7.2 4.2 %copy-start.1 = (bf16[128,7168]{1,0:T(8,128)(2,1)S(1)}, bf16[128,7168]{1,0:T(8,128)(2,1)}, u32[]{:S(2)}) copy-start(bf16[128,7168]{1,0:T(8,128)(2,1)} %param.9) | copy-start | bytes 5505028
  7.2 4.2 %copy-start.4 = (f32[7168]{0:T(1024)S(1)}, f32[7168]{0:T(1024)}, u32[]{:S(2)}) copy-start(f32[7168]{0:T(1024)} %param.10) | copy-start | bytes 86020
  7.2 4.2 %copy-start.3 = (f32[7168]{0:T(1024)S(1)}, f32[7168]{0:T(1024)}, u32[]{:S(2)}) copy-start(f32[7168]{0:T(1024)} %param.11) | copy-start | bytes 86020
  7.2 160.6 %all-gather.2.cloned.1.call-start = ((), (), s32[]{:S(2)}) async-start(), calls=%async_computation.2 | async-start | bytes 16515072 | tf_op jit(solution)/shard_map/all_gather | solution.py:91
  9.2 4.2 %copy-start.6 = (s32[64]{0:T(128)S(1)}, s32[64]{0:T(128)}, u32[]{:S(2)}) copy-start(s32[64]{0:T(128)} %param.17) | copy-start | bytes 772
  9.2 16.2 %copy-start.2 = (s32[1024]{0:T(1024)S(1)}, s32[1024]{0:T(1024)}, u32[]{:S(2)}) copy-start(s32[1024]{0:T(1024)} %param.16) | copy-start | bytes 12292
  9.2 16.8 %copy-start.5 = (f32[3,512]{1,0:T(4,128)S(1)}, f32[3,512]{1,0:T(4,128)}, u32[]{:S(2)}) copy-start(f32[3,512]{1,0:T(4,128)} %param.15) | copy-start | bytes 18436
  17.0 15.4 %all-to-all-start.1 = ((s32[16,4,1]{1,2,0:T(1,128)}), s32[16,4,1]{1,2,0:T(1,128)S(1)}, u32[]{:S(2)}, u32[]{:S(2)}) async-start(s32[16,4,1]{1,2,0:T(1,128)} %bitcast.7), calls=%async_computation.1 | async-start | bytes 16384 | tf_op jit(solution)/shard_map/all_to_all | solution.py:83
  190.3 6.7 %copy-start = (bf16[1024,1024]{1,0:T(8,128)(2,1)}, bf16[1024,1024]{1,0:T(8,128)(2,1)S(1)}, u32[]{:S(2)}) copy-start(bf16[1024,1024]{1,0:T(8,128)(2,1)S(1)} %select_convert_fusion.k_ref.v_ref) | copy-start | bytes 6291460
  200.7 35.6 %all-to-all-start = ((bf16[64,2,16,4,128]{4,2,3,1,0:T(8,128)(2,1)}), bf16[64,2,16,4,128]{4,2,3,1,0:T(8,128)(2,1)S(1)}, u32[]{:S(2)}, u32[]{:S(2)}) async-start(bf16[64,2,16,4,128]{4,2,3,1,0:T(8,128)(2,1)} %gather_fusion), calls=%async_computation | async-start | bytes 4194304 | tf_op jit(solution)/shard_map/all_to_all | solution.py:85
Sparse Core Ops, SparseCore 0:
  13.6 154.1 all-gather.1

commit v4 on v3

--- a/solution.py
+++ b/solution.py
@@ -76,14 +76,15 @@
     positions, width = kv.shape
     page_rows = positions // pages
     heads = width // (2 * HEAD_DIM)
-    stacked = kv.reshape(pages, page_rows, 2, heads, HEAD_DIM).transpose(0, 2, 1, 3, 4)
+    paged = kv.reshape(pages, page_rows, width)
     target = page_table // pages
     local_slot = page_table % pages
     order = jnp.argsort(target, stable=True)
     slots = lax.all_to_all(local_slot[order], "req", split_axis=0, concat_axis=0, tiled=True)
     inverse = jnp.argsort(slots)
-    moved = lax.all_to_all(stacked[order], "req", split_axis=0, concat_axis=0, tiled=True)
-    return moved[inverse].transpose(1, 3, 0, 2, 4)
+    moved = lax.all_to_all(paged[order], "req", split_axis=0, concat_axis=0, tiled=True)
+    placed = moved[inverse].reshape(pages, page_rows, 2, heads, HEAD_DIM)
+    return placed.transpose(2, 3, 0, 1, 4)
 
 
 def project_all(normed_local, w_query, w_key, w_value, qkv_bias, live):

time: 249 us -> 243 us (0.976)
  local copies, waits for them, and re-layouts: 20.2 us -> 14.6 us
    reshape x2 -> x1, local copies, waits for them, and re-layouts: 6.66 us -> 2.74 us  [send_pages(): placed = moved[inverse].reshape(pages, page_rows, 2, heads, HEAD_DIM)]
where the time goes in v4:
time: 243 us
  waiting for transfers between devices  138 us (57%)
  matrix products  36.4 us (15%)
  starting transfers between devices  15.7 us (6%)
  local copies, waits for them, and re-layouts  14.6 us (6%)
  between operations  14.2 us (6%)
  Pallas kernels  12.3 us (5%)
  other arithmetic  11.4 us (5%)
    all_gather x1, waiting for transfers between devices, project_all(): normed = lax.all_gather(normed_local, 'tp', axis=0, tiled=True)  132 us
    dot_general x1, matrix products, project_all(): jnp.dot(normed, w_kv, preferred_element_type=jnp.float32) + bias_kv  22.5 us
    dot_general x1, matrix products, project_all(): jnp.dot(normed, w_query, preferred_element_type=jnp.float32) + qkv_bias[0]  13.9 us
    pallas_call x1, Pallas kernels, attend(): pl.pallas_call(kernel, grid=(positions // block,), in_specs=[pl.BlockSpec...  12.3 us
    all_to_all x1, starting transfers between devices, send_pages(): lax.all_to_all(local_slot[order], 'req', split_axis=0, concat_axis=0, til...  8.44 us
    all_to_all x1, starting transfers between devices, send_pages(): lax.all_to_all(paged[order], 'req', split_axis=0, concat_axis=0, tiled=True)  7.26 us
  transfers between devices with their start and end apart: 3, of which 3 were waited for; matrix products, arithmetic and copies ran while one was open for 9% of the time, Pallas kernels for 5%

profile of v4, /device:TPU:1, one launch (start us, length us, event | category | flops | bytes accessed | tf_op | source)
XLA Modules:
  0.0 243.1 jit_solution(106055464362534342)
XLA Ops:
  7.2 1.9 convert_reduce_fusion
  9.2 2.2 fusion.6
  11.4 2.0 fusion.9
  13.5 2.0 sort.34
  15.5 0.8 gather_fusion.1
  16.3 0.7 all_to_all.12
  17.0 8.4 %all-to-all-start.1 = ((s32[16,4,1]{1,2,0:T(1,128)}), s32[16,4,1]{1,2,0:T(1,128)S(1)}, u32[]{:S(2)}, u32[]{:S(2)}) async-start(s32[16,4,1]{1,2,0:T(1,128)} %bitcast.7), calls=%async_computation.1 | async-start | bytes 16384 | tf_op jit(solution)/shard_map/all_to_all | solution.py:83
  25.6 0.3 reduce-window.9
  26.2 1.0 copy.14.lo_ref
  27.2 1.0 copy.15.hi_ref
  28.3 4.1 %all-to-all-done.1 = s32[16,4,1]{1,2,0:T(1,128)S(1)} async-done(((s32[16,4,1]{1,2,0:T(1,128)}), s32[16,4,1]{1,2,0:T(1,128)S(1)}, u32[]{:S(2)}, u32[]{:S(2)}) %all-to-all-start.1) | async-done | bytes 288 | tf_op jit(solution)/shard_map/all_to_all | solution.py:83
  32.4 0.5 broadcast.88
  32.9 0.7 reduce.5
  33.7 2.0 sort.35
  35.7 132.1 %all-gather.2.cloned.1.call-done = bf16[1024,7168]{1,0:T(8,128)(2,1)} async-done(((bf16[128,7168]{1,0:T(8,128)(2,1)}), bf16[1024,7168]{1,0:T(8,128)(2,1)}) %all-gather.2.cloned.1.call-update) | async-done | bytes 14680080 | tf_op jit(solution)/shard_map/all_gather | solution.py:92
  167.8 22.5 %select_convert_fusion.k_ref.v_ref = bf16[1024,1024]{1,0:T(8,128)(2,1)S(1)} fusion(f32[1024]{0:T(1024)S(1)} %pad_maximum_fusion, pred[1024]{0:T(1024)(128)(4,1)S(1)} %get-tuple-element.11, bf16[1024,7168]{1,0:T(8,128)(2,1)} %all-gather.2.cloned.1.call-done, bf16[7168,512]{1,0:T(8,128)(2,1)} %param.14, bf16[7168,512]{1,0:T(8,128)(2,1)} %param.13), kind=kOutput, calls=%fused_computation.11 | convolution fusion | flops 15064891392 | bytes 31462400 | tf_op jit(solution)/shard_map/dot_general | solution.py:95
  190.3 2.0 gather_fusion
  192.4 7.3 %all-to-all-start = ((bf16[64,16,1024]{2,1,0:T(8,128)(2,1)}), bf16[64,16,1024]{2,1,0:T(8,128)(2,1)}, u32[]{:S(2)}, u32[]{:S(2)}) async-start(bf16[64,16,1024]{2,1,0:T(8,128)(2,1)} %gather_fusion), calls=%async_computation | async-start | bytes 4194304 | tf_op jit(solution)/shard_map/all_to_all | solution.py:85
  199.6 13.9 %multiply_convert_fusion.q_ref = bf16[1024,512]{1,0:T(8,128)(2,1)} fusion(bf16[1024,7168]{1,0:T(8,128)(2,1)} %all-gather.2.cloned.1.call-done, bf16[7168,512]{1,0:T(8,128)(2,1)} %param.12, f32[512]{0:T(512)S(1)} %bitcast.22), kind=kOutput, calls=%fused_computation.16 | convolution fusion | flops 7517765632 | bytes 23070720 | tf_op jit(solution)/shard_map/dot_general | solution.py:98
  213.6 12.3 %shard_map.104 = bf16[1024,512]{1,0:T(8,128)(2,1)} custom-call(bf16[1024,512]{1,0:T(8,128)(2,1)} %multiply_convert_fusion.q_ref, bf16[1024,1024]{1,0:T(8,128)(2,1)} %copy-done, bf16[1024,1024]{1,0:T(8,128)(2,1)} %copy-done, s32[1024,1]{1,0:T(8,128)} %copy.14.lo_ref, s32[1024,1]{1,0:T(8,128)} %copy.15.hi_ref), custom_call_target="tpu_custom_call" | custom-call | tf_op jit(solution)/shard_map/pallas_call | solution.py:59
  225.9 2.2 all-to-all-done
  228.1 2.3 gather_fusion.2
  230.4 2.7 %reshape.68 = bf16[64,16,2,4,128]{4,3,2,1,0:T(4,128)(2,1)} reshape(bf16[64,16,1024]{2,1,0:T(8,128)(2,1)S(1)} %gather_fusion.2) | data formatting | bytes 4194304 | tf_op jit(solution)/shard_map/reshape | solution.py:86
  233.1 3.2 %copy.17 = bf16[2,4,64,16,128]{4,3,2,1,0:T(8,128)(2,1)} copy(bf16[2,4,64,16,128]{4,1,0,3,2:T(4,128)(2,1)} %bitcast.17) | data formatting | bytes 4194304
  (35 shorter events, 0.7 us)
Async XLA Ops:
  7.2 4.2 %copy-start.1 = (bf16[128,7168]{1,0:T(8,128)(2,1)S(1)}, bf16[128,7168]{1,0:T(8,128)(2,1)}, u32[]{:S(2)}) copy-start(bf16[128,7168]{1,0:T(8,128)(2,1)} %param.9) | copy-start | bytes 5505028
  7.2 4.2 %copy-start.4 = (f32[7168]{0:T(1024)S(1)}, f32[7168]{0:T(1024)}, u32[]{:S(2)}) copy-start(f32[7168]{0:T(1024)} %param.10) | copy-start | bytes 86020
  7.2 4.2 %copy-start.3 = (f32[7168]{0:T(1024)S(1)}, f32[7168]{0:T(1024)}, u32[]{:S(2)}) copy-start(f32[7168]{0:T(1024)} %param.11) | copy-start | bytes 86020
  7.2 160.6 %all-gather.2.cloned.1.call-start = ((), (), s32[]{:S(2)}) async-start(), calls=%async_computation.2 | async-start | bytes 16515072 | tf_op jit(solution)/shard_map/all_gather | solution.py:92
  9.2 4.3 %copy-start.6 = (s32[64]{0:T(128)S(1)}, s32[64]{0:T(128)}, u32[]{:S(2)}) copy-start(s32[64]{0:T(128)} %param.17) | copy-start | bytes 772
  9.2 16.2 %copy-start.2 = (s32[1024]{0:T(1024)S(1)}, s32[1024]{0:T(1024)}, u32[]{:S(2)}) copy-start(s32[1024]{0:T(1024)} %param.16) | copy-start | bytes 12292
  9.2 16.8 %copy-start.5 = (f32[3,512]{1,0:T(4,128)S(1)}, f32[3,512]{1,0:T(4,128)}, u32[]{:S(2)}) copy-start(f32[3,512]{1,0:T(4,128)} %param.15) | copy-start | bytes 18436
  17.0 15.4 %all-to-all-start.1 = ((s32[16,4,1]{1,2,0:T(1,128)}), s32[16,4,1]{1,2,0:T(1,128)S(1)}, u32[]{:S(2)}, u32[]{:S(2)}) async-start(s32[16,4,1]{1,2,0:T(1,128)} %bitcast.7), calls=%async_computation.1 | async-start | bytes 16384 | tf_op jit(solution)/shard_map/all_to_all | solution.py:83
  190.3 2.0 copy-start
  192.4 35.7 %all-to-all-start = ((bf16[64,16,1024]{2,1,0:T(8,128)(2,1)}), bf16[64,16,1024]{2,1,0:T(8,128)(2,1)}, u32[]{:S(2)}, u32[]{:S(2)}) async-start(bf16[64,16,1024]{2,1,0:T(8,128)(2,1)} %gather_fusion), calls=%async_computation | async-start | bytes 4194304 | tf_op jit(solution)/shard_map/all_to_all | solution.py:85
Sparse Core Ops, SparseCore 0:
  13.6 154.1 all-gather.1

commit v5 on v4

--- a/solution.py
+++ b/solution.py
@@ -4,6 +4,7 @@
 import jax.numpy as jnp
 from jax import lax
 from jax.experimental import pallas as pl
+from jax.experimental.pallas import tpu as pltpu
 from jax.sharding import PartitionSpec as P
 
 HEAD_DIM = 128
@@ -83,8 +84,36 @@
     slots = lax.all_to_all(local_slot[order], "req", split_axis=0, concat_axis=0, tiled=True)
     inverse = jnp.argsort(slots)
     moved = lax.all_to_all(paged[order], "req", split_axis=0, concat_axis=0, tiled=True)
-    placed = moved[inverse].reshape(pages, page_rows, 2, heads, HEAD_DIM)
-    return placed.transpose(2, 3, 0, 1, 4)
+    return place_pages(moved, inverse, heads)
+
+
+def place_kernel(inverse_ref, moved_ref, out_ref):
+    kinds, heads = out_ref.shape[0], out_ref.shape[1]
+
+    def body(slot, carry):
+        page = moved_ref[inverse_ref[slot]]
+        for k in range(kinds):
+            for h in range(heads):
+                lo = (k * heads + h) * HEAD_DIM
+                out_ref[k, h, slot] = page[:, lo : lo + HEAD_DIM]
+        return carry
+
+    lax.fori_loop(0, out_ref.shape[2], body, 0)
+
+
+def place_pages(moved, inverse, heads):
+    pages, page_rows, _ = moved.shape
+    shape = (2, heads, pages, page_rows, HEAD_DIM)
+    return pl.pallas_call(
+        place_kernel,
+        grid_spec=pltpu.PrefetchScalarGridSpec(
+            num_scalar_prefetch=1,
+            grid=(1,),
+            in_specs=[pl.BlockSpec(moved.shape, lambda i, inv: (0, 0, 0))],
+            out_specs=pl.BlockSpec(shape, lambda i, inv: (0, 0, 0, 0, 0)),
+        ),
+        out_shape=jax.ShapeDtypeStruct(shape, moved.dtype),
+    )(inverse.astype(jnp.int32), moved)
 
 
 def project_all(normed_local, w_query, w_key, w_value, qkv_bias, live):

time: 243 us -> 243 us (level)
  local copies, waits for them, and re-layouts: 14.6 us -> 6.4 us
  Pallas kernels: 12.3 us -> 16.5 us
  waiting for transfers between devices: 138 us -> 142 us
    all_gather x1, waiting for transfers between devices: 132 us -> 142 us  [project_all(): normed = lax.all_gather(normed_local, 'tp', axis=0, tiled=True)]
    pallas_call x0 -> x1, Pallas kernels: none -> 4.2 us  [place_pages(): pl.pallas_call(place_kernel, grid_spec=pltpu.PrefetchScalarGridSpec(num_s...]
    all_to_all x1, waiting for transfers between devices: 4.1 us -> 0.01 us  [send_pages(): lax.all_to_all(local_slot[order], 'req', split_axis=0, concat_axis=0, til...]
    unnamed x15 -> x14, local copies, waits for them, and re-layouts: 3.22 us -> 0.04 us
    reshape x1 -> x0, local copies, waits for them, and re-layouts: 2.74 us -> none  [send_pages(): placed = moved[inverse].reshape(pages, page_rows, 2, heads, HEAD_DIM)]
  transfers between devices with their start and end apart: 3 -> 3, of which waited for: 3 -> 1; matrix products, arithmetic and copies ran while one was open for 9% -> 20% of each run, Pallas kernels for 5% -> 5%
where the time goes in v5:
time: 243 us; the launch traced here: 242 us
  waiting for transfers between devices  142 us (58%)
  matrix products  36.4 us (15%)
  Pallas kernels  16.5 us (7%)
  starting transfers between devices  15.7 us (6%)
  between operations  14.2 us (6%)
  other arithmetic  11.5 us (5%)
  local copies, waits for them, and re-layouts  6.4 us (3%)
    all_gather x1, waiting for transfers between devices, project_all(): normed = lax.all_gather(normed_local, 'tp', axis=0, tiled=True)  142 us
    dot_general x1, matrix products, project_all(): jnp.dot(normed, w_kv, preferred_element_type=jnp.float32) + bias_kv  22.5 us
    dot_general x1, matrix products, project_all(): jnp.dot(normed, w_query, preferred_element_type=jnp.float32) + qkv_bias[0]  13.9 us
    pallas_call x1, Pallas kernels, attend(): pl.pallas_call(kernel, grid=(positions // block,), in_specs=[pl.BlockSpec...  12.3 us
    all_to_all x1, starting transfers between devices, send_pages(): lax.all_to_all(local_slot[order], 'req', split_axis=0, concat_axis=0, til...  8.44 us
    all_to_all x1, starting transfers between devices, send_pages(): lax.all_to_all(paged[order], 'req', split_axis=0, concat_axis=0, tiled=True)  7.26 us
  transfers between devices with their start and end apart: 3, of which 1 were waited for; matrix products, arithmetic and copies ran while one was open for 20% of the time, Pallas kernels for 5%

profile of v5, /device:TPU:1, one launch (start us, length us, event | category | flops | bytes accessed | tf_op | source)
XLA Modules:
  0.0 242.4 jit_solution(11849396187238711710)
XLA Ops:
  7.2 1.9 convert_reduce_fusion
  9.2 2.2 fusion.6
  11.4 2.0 fusion.9
  13.5 2.0 sort.34
  15.5 0.8 gather_fusion
  16.3 0.7 all_to_all.11
  17.0 8.4 %all-to-all-start = ((s32[16,4,1]{1,2,0:T(1,128)}), s32[16,4,1]{1,2,0:T(1,128)S(1)}, u32[]{:S(2)}, u32[]{:S(2)}) async-start(s32[16,4,1]{1,2,0:T(1,128)} %bitcast.6), calls=%async_computation | async-start | bytes 16384 | tf_op jit(solution)/shard_map/all_to_all | solution.py:84
  25.4 0.1 slice_compare_fusion
  25.5 0.1 add_select_fusion
  25.6 0.3 reduce-window.9
  26.0 0.1 slice_reduce_fusion
  26.1 141.7 %all-gather.2.cloned.1.call-done = bf16[1024,7168]{1,0:T(8,128)(2,1)} async-done(((bf16[128,7168]{1,0:T(8,128)(2,1)}), bf16[1024,7168]{1,0:T(8,128)(2,1)}) %all-gather.2.cloned.1.call-update) | async-done | bytes 14680080 | tf_op jit(solution)/shard_map/all_gather | solution.py:121
  167.8 22.5 %select_convert_fusion.k_ref.v_ref = bf16[1024,1024]{1,0:T(8,128)(2,1)S(1)} fusion(f32[1024]{0:T(1024)S(1)} %pad_maximum_fusion, pred[1024]{0:T(1024)(128)(4,1)S(1)} %get-tuple-element.7, bf16[1024,7168]{1,0:T(8,128)(2,1)} %all-gather.2.cloned.1.call-done, bf16[7168,512]{1,0:T(8,128)(2,1)} %param.14, bf16[7168,512]{1,0:T(8,128)(2,1)} %param.13), kind=kOutput, calls=%fused_computation.10 | convolution fusion | flops 15064891392 | bytes 31462400 | tf_op jit(solution)/shard_map/dot_general | solution.py:124
  190.3 2.0 gather_fusion.1
  192.4 7.3 %all-to-all-start.1 = ((bf16[64,16,1024]{2,1,0:T(8,128)(2,1)}), bf16[64,16,1024]{2,1,0:T(8,128)(2,1)}, u32[]{:S(2)}, u32[]{:S(2)}) async-start(bf16[64,16,1024]{2,1,0:T(8,128)(2,1)} %gather_fusion.1), calls=%async_computation.1 | async-start | bytes 4194304 | tf_op jit(solution)/shard_map/all_to_all | solution.py:86
  199.7 1.0 copy.13.lo_ref
  200.7 1.0 copy.14.hi_ref
  201.8 0.5 broadcast.83
  202.3 0.7 reduce.5
  203.0 0.1 all_to_all.13
  203.1 2.1 sort.35
  205.1 13.9 %multiply_convert_fusion.q_ref = bf16[1024,512]{1,0:T(8,128)(2,1)} fusion(bf16[1024,7168]{1,0:T(8,128)(2,1)} %all-gather.2.cloned.1.call-done, bf16[7168,512]{1,0:T(8,128)(2,1)} %param.12, f32[512]{0:T(512)S(1)} %bitcast.20), kind=kOutput, calls=%fused_computation.15 | convolution fusion | flops 7517765632 | bytes 23070720 | tf_op jit(solution)/shard_map/dot_general | solution.py:127
  219.0 12.3 %shard_map.104 = bf16[1024,512]{1,0:T(8,128)(2,1)} custom-call(bf16[1024,512]{1,0:T(8,128)(2,1)} %multiply_convert_fusion.q_ref, bf16[1024,1024]{1,0:T(8,128)(2,1)} %copy-done, bf16[1024,1024]{1,0:T(8,128)(2,1)} %copy-done, s32[1024,1]{1,0:T(8,128)} %copy.13.lo_ref, s32[1024,1]{1,0:T(8,128)} %copy.14.hi_ref), custom_call_target="tpu_custom_call" | custom-call | tf_op jit(solution)/shard_map/pallas_call | solution.py:60
  231.3 4.2 %shard_map.105 = bf16[2,4,64,16,128]{4,3,2,1,0:T(8,128)(2,1)} custom-call(s32[64]{0:T(128)} %get-tuple-element.5.inverse_ref, bf16[64,16,1024]{2,1,0:T(8,128)(2,1)} %all-to-all-done.1.moved_ref), custom_call_target="tpu_custom_call" | custom-call | tf_op jit(solution)/shard_map/pallas_call | solution.py:107
  (31 shorter events, 0.3 us)
Async XLA Ops:
  7.2 4.2 %copy-start.1 = (bf16[128,7168]{1,0:T(8,128)(2,1)S(1)}, bf16[128,7168]{1,0:T(8,128)(2,1)}, u32[]{:S(2)}) copy-start(bf16[128,7168]{1,0:T(8,128)(2,1)} %param.9) | copy-start | bytes 5505028
  7.2 4.2 %copy-start.4 = (f32[7168]{0:T(1024)S(1)}, f32[7168]{0:T(1024)}, u32[]{:S(2)}) copy-start(f32[7168]{0:T(1024)} %param.10) | copy-start | bytes 86020
  7.2 4.2 %copy-start.3 = (f32[7168]{0:T(1024)S(1)}, f32[7168]{0:T(1024)}, u32[]{:S(2)}) copy-start(f32[7168]{0:T(1024)} %param.11) | copy-start | bytes 86020
  7.2 160.6 %all-gather.2.cloned.1.call-start = ((), (), s32[]{:S(2)}) async-start(), calls=%async_computation.2 | async-start | bytes 16515072 | tf_op jit(solution)/shard_map/all_gather | solution.py:121
  9.2 4.3 %copy-start.6 = (s32[64]{0:T(128)S(1)}, s32[64]{0:T(128)}, u32[]{:S(2)}) copy-start(s32[64]{0:T(128)} %param.17) | copy-start | bytes 772
  9.2 16.2 %copy-start.2 = (s32[1024]{0:T(1024)S(1)}, s32[1024]{0:T(1024)}, u32[]{:S(2)}) copy-start(s32[1024]{0:T(1024)} %param.16) | copy-start | bytes 12292
  9.2 16.8 %copy-start.5 = (f32[3,512]{1,0:T(4,128)S(1)}, f32[3,512]{1,0:T(4,128)}, u32[]{:S(2)}) copy-start(f32[3,512]{1,0:T(4,128)} %param.15) | copy-start | bytes 18436
  17.0 175.4 %all-to-all-start = ((s32[16,4,1]{1,2,0:T(1,128)}), s32[16,4,1]{1,2,0:T(1,128)S(1)}, u32[]{:S(2)}, u32[]{:S(2)}) async-start(s32[16,4,1]{1,2,0:T(1,128)} %bitcast.6), calls=%async_computation | async-start | bytes 16384 | tf_op jit(solution)/shard_map/all_to_all | solution.py:84
  190.3 2.0 copy-start
  192.4 39.0 %all-to-all-start.1 = ((bf16[64,16,1024]{2,1,0:T(8,128)(2,1)}), bf16[64,16,1024]{2,1,0:T(8,128)(2,1)}, u32[]{:S(2)}, u32[]{:S(2)}) async-start(bf16[64,16,1024]{2,1,0:T(8,128)(2,1)} %gather_fusion.1), calls=%async_computation.1 | async-start | bytes 4194304 | tf_op jit(solution)/shard_map/all_to_all | solution.py:86
Sparse Core Ops, SparseCore 0:
  13.6 154.1 all-gather.1

commit v6 on v5

--- a/solution.py
+++ b/solution.py
@@ -8,7 +8,7 @@
 from jax.sharding import PartitionSpec as P
 
 HEAD_DIM = 128
-Q_BLOCK = 256
+Q_BLOCK = 512
 
 
 def layer_norm(rows, gain, shift):
@@ -54,8 +54,8 @@
     block = Q_BLOCK
     position = jnp.arange(positions, dtype=jnp.int32)
     first = jnp.concatenate([jnp.ones((1,), bool), segments[1:] != segments[:-1]])
-    lo = lax.cummax(jnp.where(first, position, 0), axis=0)
-    hi = jnp.where(segments >= 0, position, -1)
+    lo = lax.cummax(jnp.where(first, position, 0), axis=0).reshape(positions, 1)
+    hi = jnp.where(segments >= 0, position, -1).reshape(positions, 1)
     kernel = functools.partial(attention_kernel, block=block)
     return pl.pallas_call(
         kernel,
@@ -69,7 +69,7 @@
         ],
         out_specs=pl.BlockSpec((block, width), lambda i: (i, 0)),
         out_shape=jax.ShapeDtypeStruct((positions, width), query.dtype),
-    )(query, kv, kv, lo.reshape(positions, 1), hi.reshape(positions, 1))
+    )(query, kv, kv, lo, hi)
 
 
 def send_pages(kv, page_table):

time: 243 us -> 241 us (level)
  transfers between devices with their start and end apart: 3 -> 3, of which waited for: 1 -> 1; matrix products, arithmetic and copies ran while one was open for 20% -> 20% of each run, Pallas kernels for 5% -> 4%
where the time goes in v6:
time: 241 us; the launch traced here: 240 us
  waiting for transfers between devices  142 us (59%)
  matrix products  36.4 us (15%)
  starting transfers between devices  15.7 us (7%)
  Pallas kernels  14.4 us (6%)
  between operations  14.2 us (6%)
  other arithmetic  11.5 us (5%)
  local copies, waits for them, and re-layouts  6.4 us (3%)
    all_gather x1, waiting for transfers between devices, project_all(): normed = lax.all_gather(normed_local, 'tp', axis=0, tiled=True)  142 us
    dot_general x1, matrix products, project_all(): jnp.dot(normed, w_kv, preferred_element_type=jnp.float32) + bias_kv  22.5 us
    dot_general x1, matrix products, project_all(): jnp.dot(normed, w_query, preferred_element_type=jnp.float32) + qkv_bias[0]  13.9 us
    pallas_call x1, Pallas kernels, attend(): pl.pallas_call(kernel, grid=(positions // block,), in_specs=[pl.BlockSpec...  10.2 us
    all_to_all x1, starting transfers between devices, send_pages(): lax.all_to_all(local_slot[order], 'req', split_axis=0, concat_axis=0, til...  8.44 us
    all_to_all x1, starting transfers between devices, send_pages(): lax.all_to_all(paged[order], 'req', split_axis=0, concat_axis=0, tiled=True)  7.26 us
  transfers between devices with their start and end apart: 3, of which 1 were waited for; matrix products, arithmetic and copies ran while one was open for 20% of the time, Pallas kernels for 4%

profile of v6, /device:TPU:1, one launch (start us, length us, event | category | flops | bytes accessed | tf_op | source)
XLA Modules:
  0.0 240.3 jit_solution(15904911496542261218)
XLA Ops:
  7.2 1.9 convert_reduce_fusion
  9.2 2.2 fusion.6
  11.4 2.0 fusion.9
  13.5 2.0 sort.34
  15.5 0.8 gather_fusion
  16.3 0.7 all_to_all.11
  17.0 8.4 %all-to-all-start = ((s32[16,4,1]{1,2,0:T(1,128)}), s32[16,4,1]{1,2,0:T(1,128)S(1)}, u32[]{:S(2)}, u32[]{:S(2)}) async-start(s32[16,4,1]{1,2,0:T(1,128)} %bitcast.6), calls=%async_computation | async-start | bytes 16384 | tf_op jit(solution)/shard_map/all_to_all | solution.py:84
  25.4 0.1 slice_compare_fusion
  25.5 0.1 add_select_fusion
  25.6 0.3 reduce-window.9
  26.0 0.1 slice_reduce_fusion
  26.1 141.7 %all-gather.2.cloned.1.call-done = bf16[1024,7168]{1,0:T(8,128)(2,1)} async-done(((bf16[128,7168]{1,0:T(8,128)(2,1)}), bf16[1024,7168]{1,0:T(8,128)(2,1)}) %all-gather.2.cloned.1.call-update) | async-done | bytes 14680080 | tf_op jit(solution)/shard_map/all_gather | solution.py:121
  167.8 22.5 %select_convert_fusion.k_ref.v_ref = bf16[1024,1024]{1,0:T(8,128)(2,1)S(1)} fusion(f32[1024]{0:T(1024)S(1)} %pad_maximum_fusion, pred[1024]{0:T(1024)(128)(4,1)S(1)} %get-tuple-element.7, bf16[1024,7168]{1,0:T(8,128)(2,1)} %all-gather.2.cloned.1.call-done, bf16[7168,512]{1,0:T(8,128)(2,1)} %param.14, bf16[7168,512]{1,0:T(8,128)(2,1)} %param.13), kind=kOutput, calls=%fused_computation.10 | convolution fusion | flops 15064891392 | bytes 31462400 | tf_op jit(solution)/shard_map/dot_general | solution.py:124
  190.3 2.0 gather_fusion.1
  192.4 7.3 %all-to-all-start.1 = ((bf16[64,16,1024]{2,1,0:T(8,128)(2,1)}), bf16[64,16,1024]{2,1,0:T(8,128)(2,1)}, u32[]{:S(2)}, u32[]{:S(2)}) async-start(bf16[64,16,1024]{2,1,0:T(8,128)(2,1)} %gather_fusion.1), calls=%async_computation.1 | async-start | bytes 4194304 | tf_op jit(solution)/shard_map/all_to_all | solution.py:86
  199.7 1.0 copy.13.lo_ref
  200.7 1.0 copy.14.hi_ref
  201.8 0.5 broadcast.83
  202.3 0.7 reduce.5
  203.0 0.1 all_to_all.13
  203.1 2.1 sort.35
  205.1 13.9 %multiply_convert_fusion.q_ref = bf16[1024,512]{1,0:T(8,128)(2,1)} fusion(bf16[1024,7168]{1,0:T(8,128)(2,1)} %all-gather.2.cloned.1.call-done, bf16[7168,512]{1,0:T(8,128)(2,1)} %param.12, f32[512]{0:T(512)S(1)} %bitcast.20), kind=kOutput, calls=%fused_computation.15 | convolution fusion | flops 7517765632 | bytes 23070720 | tf_op jit(solution)/shard_map/dot_general | solution.py:127
  219.0 10.2 %shard_map.104 = bf16[1024,512]{1,0:T(8,128)(2,1)} custom-call(bf16[1024,512]{1,0:T(8,128)(2,1)} %multiply_convert_fusion.q_ref, bf16[1024,1024]{1,0:T(8,128)(2,1)} %copy-done, bf16[1024,1024]{1,0:T(8,128)(2,1)} %copy-done, s32[1024,1]{1,0:T(8,128)} %copy.13.lo_ref, s32[1024,1]{1,0:T(8,128)} %copy.14.hi_ref), custom_call_target="tpu_custom_call" | custom-call | tf_op jit(solution)/shard_map/pallas_call | solution.py:60
  229.3 4.2 %shard_map.105 = bf16[2,4,64,16,128]{4,3,2,1,0:T(8,128)(2,1)} custom-call(s32[64]{0:T(128)} %get-tuple-element.5.inverse_ref, bf16[64,16,1024]{2,1,0:T(8,128)(2,1)} %all-to-all-done.1.moved_ref), custom_call_target="tpu_custom_call" | custom-call | tf_op jit(solution)/shard_map/pallas_call | solution.py:107
  (31 shorter events, 0.3 us)
Async XLA Ops:
  7.2 4.2 %copy-start.1 = (bf16[128,7168]{1,0:T(8,128)(2,1)S(1)}, bf16[128,7168]{1,0:T(8,128)(2,1)}, u32[]{:S(2)}) copy-start(bf16[128,7168]{1,0:T(8,128)(2,1)} %param.9) | copy-start | bytes 5505028
  7.2 4.2 %copy-start.4 = (f32[7168]{0:T(1024)S(1)}, f32[7168]{0:T(1024)}, u32[]{:S(2)}) copy-start(f32[7168]{0:T(1024)} %param.10) | copy-start | bytes 86020
  7.2 4.2 %copy-start.3 = (f32[7168]{0:T(1024)S(1)}, f32[7168]{0:T(1024)}, u32[]{:S(2)}) copy-start(f32[7168]{0:T(1024)} %param.11) | copy-start | bytes 86020
  7.2 160.6 %all-gather.2.cloned.1.call-start = ((), (), s32[]{:S(2)}) async-start(), calls=%async_computation.2 | async-start | bytes 16515072 | tf_op jit(solution)/shard_map/all_gather | solution.py:121
  9.2 4.3 %copy-start.6 = (s32[64]{0:T(128)S(1)}, s32[64]{0:T(128)}, u32[]{:S(2)}) copy-start(s32[64]{0:T(128)} %param.17) | copy-start | bytes 772
  9.2 16.2 %copy-start.2 = (s32[1024]{0:T(1024)S(1)}, s32[1024]{0:T(1024)}, u32[]{:S(2)}) copy-start(s32[1024]{0:T(1024)} %param.16) | copy-start | bytes 12292
  9.2 16.8 %copy-start.5 = (f32[3,512]{1,0:T(4,128)S(1)}, f32[3,512]{1,0:T(4,128)}, u32[]{:S(2)}) copy-start(f32[3,512]{1,0:T(4,128)} %param.15) | copy-start | bytes 18436
  17.0 175.4 %all-to-all-start = ((s32[16,4,1]{1,2,0:T(1,128)}), s32[16,4,1]{1,2,0:T(1,128)S(1)}, u32[]{:S(2)}, u32[]{:S(2)}) async-start(s32[16,4,1]{1,2,0:T(1,128)} %bitcast.6), calls=%async_computation | async-start | bytes 16384 | tf_op jit(solution)/shard_map/all_to_all | solution.py:84
  190.3 2.0 copy-start
  192.4 36.9 %all-to-all-start.1 = ((bf16[64,16,1024]{2,1,0:T(8,128)(2,1)}), bf16[64,16,1024]{2,1,0:T(8,128)(2,1)}, u32[]{:S(2)}, u32[]{:S(2)}) async-start(bf16[64,16,1024]{2,1,0:T(8,128)(2,1)} %gather_fusion.1), calls=%async_computation.1 | async-start | bytes 4194304 | tf_op jit(solution)/shard_map/all_to_all | solution.py:86
Sparse Core Ops, SparseCore 0:
  13.6 154.1 all-gather.1

commit v7 on v6

--- a/solution.py
+++ b/solution.py
@@ -9,13 +9,30 @@
 
 HEAD_DIM = 128
 Q_BLOCK = 512
+LN_BLOCK = 64
+
+
+def layer_norm_kernel(x_ref, g_ref, b_ref, o_ref):
+    values = x_ref[...].astype(jnp.float32)
+    center = values - jnp.mean(values, axis=1, keepdims=True)
+    spread = jnp.mean(center * center, axis=1, keepdims=True)
+    o_ref[...] = (center * lax.rsqrt(spread + 1e-05) * g_ref[...] + b_ref[...]).astype(o_ref.dtype)
 
 
 def layer_norm(rows, gain, shift):
-    values = rows.astype(jnp.float32)
-    center = values - jnp.mean(values, axis=1, keepdims=True)
-    spread = jnp.mean(center * center, axis=1, keepdims=True)
-    return (center * lax.rsqrt(spread + 1e-05) * gain + shift).astype(jnp.bfloat16)
+    count, width = rows.shape
+    block = LN_BLOCK
+    return pl.pallas_call(
+        layer_norm_kernel,
+        grid=(count // block,),
+        in_specs=[
+            pl.BlockSpec((block, width), lambda i: (i, 0)),
+            pl.BlockSpec((1, width), lambda i: (0, 0)),
+            pl.BlockSpec((1, width), lambda i: (0, 0)),
+        ],
+        out_specs=pl.BlockSpec((block, width), lambda i: (i, 0)),
+        out_shape=jax.ShapeDtypeStruct((count, width), jnp.bfloat16),
+    )(rows, gain.reshape(1, width), shift.reshape(1, width))
 
 
 def attention_kernel(q_ref, k_ref, v_ref, lo_ref, hi_ref, o_ref, *, block):

time: 241 us -> 239 us (level)
  Pallas kernels: 14.4 us -> 18.5 us
  other arithmetic: 11.5 us -> 7.45 us
  waiting for transfers between devices: 142 us -> 139 us
    reduce_sum x2 -> x0, other arithmetic: 4.09 us -> none  [the longest x1 2.15 us: layer_norm(): spread = jnp.mean(center * center, axis=1, keepdims=True)]
    pallas_call x0 -> x1, Pallas kernels: none -> 4.03 us  [layer_norm(): pl.pallas_call(layer_norm_kernel, grid=(count // block,), in_specs=[pl.Bl...]
    all_gather x1, waiting for transfers between devices: 142 us -> 139 us  [project_all(): normed = lax.all_gather(normed_local, 'tp', axis=0, tiled=True)]
  transfers between devices with their start and end apart: 3 -> 3, of which waited for: 1 -> 1; matrix products, arithmetic and copies ran while one was open for 20% -> 21% of each run, Pallas kernels for 4% -> 4%
where the time goes in v7:
time: 239 us; the launch traced here: 238 us
  waiting for transfers between devices  139 us (58%)
  matrix products  36.4 us (15%)
  Pallas kernels  18.5 us (8%)
  starting transfers between devices  15.7 us (7%)
  between operations  14.1 us (6%)
  other arithmetic  7.45 us (3%)
  local copies, waits for them, and re-layouts  7.18 us (3%)
    all_gather x1, waiting for transfers between devices, project_all(): normed = lax.all_gather(normed_local, 'tp', axis=0, tiled=True)  139 us
    dot_general x1, matrix products, project_all(): jnp.dot(normed, w_kv, preferred_element_type=jnp.float32) + bias_kv  22.5 us
    dot_general x1, matrix products, project_all(): jnp.dot(normed, w_query, preferred_element_type=jnp.float32) + qkv_bias[0]  13.9 us
    pallas_call x1, Pallas kernels, attend(): pl.pallas_call(kernel, grid=(positions // block,), in_specs=[pl.BlockSpec...  10.2 us
    all_to_all x1, starting transfers between devices, send_pages(): lax.all_to_all(local_slot[order], 'req', split_axis=0, concat_axis=0, til...  8.44 us
    all_to_all x1, starting transfers between devices, send_pages(): lax.all_to_all(paged[order], 'req', split_axis=0, concat_axis=0, tiled=True)  7.27 us
  transfers between devices with their start and end apart: 3, of which 1 were waited for; matrix products, arithmetic and copies ran while one was open for 21% of the time, Pallas kernels for 4%

profile of v7, /device:TPU:1, one launch (start us, length us, event | category | flops | bytes accessed | tf_op | source)
XLA Modules:
  0.0 238.1 jit_solution(110266681097508788)
XLA Ops:
  7.2 4.0 %shard_map.104 = bf16[128,7168]{1,0:T(8,128)(2,1)} custom-call(bf16[128,7168]{1,0:T(8,128)(2,1)} %x_ref.1, f32[1,7168]{1,0:T(1,128)} %bitcast.18, f32[1,7168]{1,0:T(1,128)} %bitcast.19), custom_call_target="tpu_custom_call" | custom-call | tf_op jit(solution)/shard_map/pallas_call | solution.py:25
  11.3 0.7 and_select_fusion
  11.9 2.0 sort.34
  14.0 0.8 gather_fusion
  14.8 0.7 all_to_all.11
  15.5 8.4 %all-to-all-start = ((s32[16,4,1]{1,2,0:T(1,128)}), s32[16,4,1]{1,2,0:T(1,128)S(1)}, u32[]{:S(2)}, u32[]{:S(2)}) async-start(s32[16,4,1]{1,2,0:T(1,128)} %bitcast.8), calls=%async_computation | async-start | bytes 16384 | tf_op jit(solution)/shard_map/all_to_all | solution.py:101
  23.9 0.8 slice_compare_fusion
  24.8 0.3 reduce-window.9
  25.2 0.8 fusion.7
  26.0 0.1 slice_reduce_fusion
  26.1 0.7 iota_select_fusion
  26.8 138.8 %all-gather.2.cloned.1.call-done = bf16[1024,7168]{1,0:T(8,128)(2,1)} async-done(((bf16[128,7168]{1,0:T(8,128)(2,1)}), bf16[1024,7168]{1,0:T(8,128)(2,1)}) %all-gather.2.cloned.1.call-update) | async-done | bytes 14680080 | tf_op jit(solution)/shard_map/all_gather | solution.py:138
  165.6 22.5 %select_convert_fusion.k_ref.v_ref = bf16[1024,1024]{1,0:T(8,128)(2,1)S(1)} fusion(f32[1024]{0:T(1024)S(1)} %pad_maximum_fusion, pred[1024]{0:T(1024)(128)(4,1)S(1)} %get-tuple-element.7, bf16[1024,7168]{1,0:T(8,128)(2,1)} %all-gather.2.cloned.1.call-done, bf16[7168,512]{1,0:T(8,128)(2,1)} %param.14, bf16[7168,512]{1,0:T(8,128)(2,1)} %param.13), kind=kOutput, calls=%fused_computation.6 | convolution fusion | flops 15064891392 | bytes 31462400 | tf_op jit(solution)/shard_map/dot_general | solution.py:141
  188.1 2.0 gather_fusion.1
  190.2 7.3 %all-to-all-start.1 = ((bf16[64,16,1024]{2,1,0:T(8,128)(2,1)}), bf16[64,16,1024]{2,1,0:T(8,128)(2,1)}, u32[]{:S(2)}, u32[]{:S(2)}) async-start(bf16[64,16,1024]{2,1,0:T(8,128)(2,1)} %gather_fusion.1), calls=%async_computation.1 | async-start | bytes 4194304 | tf_op jit(solution)/shard_map/all_to_all | solution.py:103
  197.5 1.0 copy.13.lo_ref
  198.5 1.0 copy.14.hi_ref
  199.6 0.5 broadcast.58
  200.1 0.7 reduce.5
  200.8 0.1 all_to_all.13
  200.9 2.1 sort.35
  202.9 13.9 %multiply_convert_fusion.q_ref = bf16[1024,512]{1,0:T(8,128)(2,1)} fusion(bf16[1024,7168]{1,0:T(8,128)(2,1)} %all-gather.2.cloned.1.call-done, bf16[7168,512]{1,0:T(8,128)(2,1)} %param.12, f32[512]{0:T(512)S(1)} %bitcast.24), kind=kOutput, calls=%fused_computation.7 | convolution fusion | flops 7517765632 | bytes 23070720 | tf_op jit(solution)/shard_map/dot_general | solution.py:144
  216.9 10.2 %shard_map.105 = bf16[1024,512]{1,0:T(8,128)(2,1)} custom-call(bf16[1024,512]{1,0:T(8,128)(2,1)} %multiply_convert_fusion.q_ref, bf16[1024,1024]{1,0:T(8,128)(2,1)} %copy-done, bf16[1024,1024]{1,0:T(8,128)(2,1)} %copy-done, s32[1024,1]{1,0:T(8,128)} %copy.13.lo_ref, s32[1024,1]{1,0:T(8,128)} %copy.14.hi_ref), custom_call_target="tpu_custom_call" | custom-call | tf_op jit(solution)/shard_map/pallas_call | solution.py:77
  227.1 4.2 %shard_map.106 = bf16[2,4,64,16,128]{4,3,2,1,0:T(8,128)(2,1)} custom-call(s32[64]{0:T(128)} %get-tuple-element.5.inverse_ref, bf16[64,16,1024]{2,1,0:T(8,128)(2,1)} %all-to-all-done.1.moved_ref), custom_call_target="tpu_custom_call" | custom-call | tf_op jit(solution)/shard_map/pallas_call | solution.py:124
  (15 shorter events, 0.3 us)
Async XLA Ops:
  7.2 158.5 %all-gather.2.cloned.1.call-start = ((), (), s32[]{:S(2)}) async-start(), calls=%async_computation.2 | async-start | bytes 16515072 | tf_op jit(solution)/shard_map/all_gather | solution.py:138
  15.5 174.7 %all-to-all-start = ((s32[16,4,1]{1,2,0:T(1,128)}), s32[16,4,1]{1,2,0:T(1,128)S(1)}, u32[]{:S(2)}, u32[]{:S(2)}) async-start(s32[16,4,1]{1,2,0:T(1,128)} %bitcast.8), calls=%async_computation | async-start | bytes 16384 | tf_op jit(solution)/shard_map/all_to_all | solution.py:101
  188.1 28.7 %copy-start = (bf16[1024,1024]{1,0:T(8,128)(2,1)}, bf16[1024,1024]{1,0:T(8,128)(2,1)S(1)}, u32[]{:S(2)}) copy-start(bf16[1024,1024]{1,0:T(8,128)(2,1)S(1)} %select_convert_fusion.k_ref.v_ref) | copy-start | bytes 6291460
  190.2 36.9 %all-to-all-start.1 = ((bf16[64,16,1024]{2,1,0:T(8,128)(2,1)}), bf16[64,16,1024]{2,1,0:T(8,128)(2,1)}, u32[]{:S(2)}, u32[]{:S(2)}) async-start(bf16[64,16,1024]{2,1,0:T(8,128)(2,1)} %gather_fusion.1), calls=%async_computation.1 | async-start | bytes 4194304 | tf_op jit(solution)/shard_map/all_to_all | solution.py:103
Sparse Core Ops, SparseCore 0:
  11.4 154.2 all-gather.1
